TPU v7x, 32 devices: a whole 2x2x4 slice. The times are simulated.
32 devices in a mesh: region: 4 (over z), tok: 8 (over y, x, core).
Axes of the slice: x: 2, y: 2, z: 4, core: 2. Of those that a mesh axis runs over, the one named last changes fastest.
Arguments:
- tokens: bfloat16 [4096, 1024], P(('region', 'tok')), may hold values from -6 to 6
- w_query: bfloat16 [1024, 1024], P('tok'), may hold values from -0.1875 to 0.1875
- w_key: bfloat16 [1024, 1024], P('tok'), may hold values from -0.1875 to 0.1875
- w_value: bfloat16 [1024, 1024], P('tok'), may hold values from -0.1875 to 0.1875
- w_out: bfloat16 [1024, 1024], P(None, 'tok'), may hold values from -0.1875 to 0.1875
- past_keys: bfloat16 [4, 4096, 1024], P(None, ('region', 'tok')), may hold values from -600 to 600
- past_values: bfloat16 [4, 4096, 1024], P(None, ('region', 'tok')), may hold values from -6 to 6
- nb_block: int32 [32, 8], replicated, may hold values from 0 to 31, as said below
- nb_frame: int32 [32, 8], replicated, may hold values from 0 to 3, as said below
- nb_count: int32 [32], replicated, may hold values from 2 to 8
- block_slot: int32 [32], replicated, may hold values from 0 to 31, as said below
Outputs:
- attn_out: bfloat16 [4096, 1024], P(('region', 'tok'))
Inputs may be any that keep to these rules, and one draw needn't show every extreme that they name: block_slot is a permutation of the block ids; device i of region+tok stores slot i (one block per device). `nb_block`: the entries of one query block name distinct blocks. For the query blocks of device (r, c) of region+tok, entry 0 names one and the same block and frame stored in region group r - 1, entry 1 one and the same stored in group r + 1 (periodic), the other entries blocks stored in group r, on tok indices other than those of entries 0 and 1. For each group r and tok index t, exactly one device of group r reads its entry 0 from tok index t of group r - 1, and exactly one reads its entry 1 from tok index t of group r + 1. All entries of query blocks of devices with tok index c that name blocks stored on one device name one and the same block and frame. `nb_frame`: see nb_block.
All inputs are finite; a program needn't handle non-finite values.
Results may differ from a plain program's by a relative error of at most 0.0035.
The roundings to bfloat16 on the way count: a program that leaves them out, or rounds other values in their place, can miss the bound.
Values may be sent and summed in bfloat16 or wider, within the bound.
No kernel may reach another device: no remote copies, remote signals or barrier semaphores. Data moves between devices by JAX's collectives and lax.ppermute only.
A program may use at most 128 MiB of HBM per device.

v0:
```python
import jax
import jax.numpy as jnp
from jax import lax
from jax.sharding import PartitionSpec as P

HEADS = 8
QB = 128


def shifted(block, axis, distance):
    devices = range(lax.axis_size(axis))
    route = [((i - distance) % len(devices), i) for i in devices]
    return lax.ppermute(block, axis, route)


def per_device(
    tokens,
    w_query,
    w_key,
    w_value,
    w_out,
    past_keys,
    past_values,
    nb_block,
    nb_frame,
    nb_count,
    block_slot,
):
    n_region = lax.axis_size("region")
    n_tok = lax.axis_size("tok")
    region_id = lax.axis_index("region")
    tok_id = lax.axis_index("tok")
    n_devices = n_region * n_tok
    my_device = region_id * n_tok + tok_id
    tok_rows, model_width = tokens.shape
    blocks_dev = tok_rows // QB
    n_blocks, max_entries = nb_block.shape
    head_size = model_width // HEADS
    whole_query, whole_key, whole_value = (
        lax.all_gather(w_query, "tok", axis=0, tiled=True),
        lax.all_gather(w_key, "tok", axis=0, tiled=True),
        lax.all_gather(w_value, "tok", axis=0, tiled=True),
    )
    proj_query = jnp.dot(tokens, whole_query, preferred_element_type=jnp.float32)
    proj_key = jnp.dot(tokens, whole_key, preferred_element_type=jnp.float32)
    proj_value = jnp.dot(tokens, whole_value, preferred_element_type=jnp.float32)
    queries = proj_query.astype(jnp.bfloat16)
    keys_new = proj_key.astype(jnp.bfloat16)
    values_new = proj_value.astype(jnp.bfloat16)
    slot_table = jnp.take(block_slot, nb_block, axis=0)
    source_dev = slot_table // blocks_dev
    source_tok = source_dev % n_tok
    flat_table = nb_frame * blocks_dev + slot_table % blocks_dev
    live_table = jnp.arange(max_entries, dtype=jnp.int32)[None, :] < nb_count[:, None]
    dest_tok = jnp.arange(n_blocks, dtype=jnp.int32) // blocks_dev % n_tok
    tok_range = jnp.arange(n_tok, dtype=jnp.int32)
    mine_flat = (live_table & (source_dev == my_device)).reshape(-1)
    dest_flat = jnp.broadcast_to(dest_tok[:, None], (n_blocks, max_entries)).reshape(-1)
    matches = mine_flat[None, :] & (dest_flat[None, :] == tok_range[:, None])
    offer_index = jnp.max(jnp.where(matches, flat_table.reshape(-1)[None, :], 0), axis=1)
    offer_keys = jnp.take(past_keys, offer_index, axis=0)
    offer_values = jnp.take(past_values, offer_index, axis=0)
    lead_tok = source_tok.reshape(n_devices, blocks_dev, max_entries)[:, 0, :2]
    lower_region = (region_id + n_region - 1) % n_region
    upper_region = (region_id + 1) % n_region
    my_start = my_device * blocks_dev
    my_tok_table = lax.dynamic_slice_in_dim(source_tok, my_start, blocks_dev, 0)
    got_keys, got_values = (
        lax.all_to_all(offer_keys, "tok", split_axis=0, concat_axis=0, tiled=True),
        lax.all_to_all(offer_values, "tok", split_axis=0, concat_axis=0, tiled=True),
    )
    upward_index = lax.dynamic_index_in_dim(
        lead_tok[:, 0], upper_region * n_tok + tok_id, 0, keepdims=False
    )
    downward_index = lax.dynamic_index_in_dim(
        lead_tok[:, 1], lower_region * n_tok + tok_id, 0, keepdims=False
    )
    upward_pair = jnp.concatenate(
        [
            lax.dynamic_slice_in_dim(got_keys, upward_index, 1, 0),
            lax.dynamic_slice_in_dim(got_values, upward_index, 1, 0),
        ],
        0,
    )
    downward_pair = jnp.concatenate(
        [
            lax.dynamic_slice_in_dim(got_keys, downward_index, 1, 0),
            lax.dynamic_slice_in_dim(got_values, downward_index, 1, 0),
        ],
        0,
    )
    below_pair = shifted(upward_pair, "region", 1)
    above_pair = shifted(downward_pair, "region", -1)
    own_index = my_tok_table[:, 2:].reshape(-1)
    own_keys = jnp.take(got_keys, own_index, axis=0).reshape(
        blocks_dev, (max_entries - 2) * QB, model_width
    )
    own_values = jnp.take(got_values, own_index, axis=0).reshape(
        blocks_dev, (max_entries - 2) * QB, model_width
    )
    side_keys = jnp.concatenate([below_pair[0], above_pair[0]], 0)[None]
    side_values = jnp.concatenate([below_pair[1], above_pair[1]], 0)[None]
    far_keys = jnp.concatenate([side_keys, own_keys], 1)
    far_values = jnp.concatenate([side_values, own_values], 1)
    key_list = jnp.concatenate([keys_new.reshape(blocks_dev, QB, model_width), far_keys], 1)
    value_list = jnp.concatenate([values_new.reshape(blocks_dev, QB, model_width), far_values], 1)
    list_len = key_list.shape[1]
    query_heads = queries.reshape(blocks_dev, QB, HEADS, head_size)
    key_heads = key_list.reshape(blocks_dev, list_len, HEADS, head_size)
    value_heads = value_list.reshape(blocks_dev, list_len, HEADS, head_size)
    attn_scale = head_size ** (-0.5)
    scores = (
        jnp.einsum("bqhd,bkhd->bhqk", query_heads, key_heads, preferred_element_type=jnp.float32)
        * attn_scale
    )
    my_counts = lax.dynamic_slice_in_dim(nb_count, my_start, blocks_dev, 0)
    entry_live = jnp.arange(max_entries, dtype=jnp.int32)[None, :] < my_counts[:, None]
    live_mask = jnp.concatenate(
        [jnp.ones((blocks_dev, QB), bool), jnp.repeat(entry_live, QB, axis=1)], 1
    )
    scores = jnp.where(live_mask[:, None, None, :], scores, jnp.float32(-1e30))
    row_max = jnp.max(scores, axis=-1, keepdims=True)
    exp_weights = jnp.where(
        live_mask[:, None, None, :], jnp.exp(scores - row_max), jnp.float32(0.0)
    )
    row_total = jnp.sum(exp_weights, axis=-1)
    prob_bf = exp_weights.astype(jnp.bfloat16)
    context = jnp.einsum(
        "bhqk,bkhd->bqhd", prob_bf, value_heads, preferred_element_type=jnp.float32
    )
    context = context / jnp.swapaxes(row_total, 1, 2)[:, :, :, None]
    context_bf = context.reshape(tok_rows, model_width).astype(jnp.bfloat16)
    whole_out = lax.all_gather(w_out, "tok", axis=1, tiled=True)
    mixed_out = jnp.dot(context_bf, whole_out, preferred_element_type=jnp.float32)
    return mixed_out.astype(jnp.bfloat16)


def solution(mesh):
    return jax.shard_map(
        per_device,
        mesh=mesh,
        in_specs=(
            P(("region", "tok"), None),
            P("tok", None),
            P("tok", None),
            P("tok", None),
            P(None, "tok"),
            P(None, ("region", "tok"), None),
            P(None, ("region", "tok"), None),
            P(),
            P(),
            P(),
            P(),
        ),
        out_specs=P(("region", "tok"), None),
        check_vma=False,
    )
```

profile of v0, /device:TPU:0, one launch (start us, length us, event | category | flops | bytes accessed | tf_op | source)
XLA Modules:
  0.0 164.5 jit_solution(5004245826716925079)
XLA Ops:
  6.5 0.7 all-gather.9.cloned.1.call-update
  7.3 0.0 all-gather.5.cloned.1.call-start
  7.3 0.7 all-gather.5.cloned.1.call-update
  8.0 0.0 all-gather.7.cloned.1.call-start
  8.1 0.7 all-gather.7.cloned.1.call-update
  8.8 0.8 copy.48
  9.5 0.1 reshape.191
  9.6 0.0 copy-start.5
  9.7 1.9 %gather_fusion = s32[256]{0:T(256)S(1)} fusion(s32[32]{0:T(128)S(1)} %copy-done.1, s32[1024]{0:T(1024)S(1)} %pad_clamp_fusion.2), kind=kCustom, calls=%fused_computation.4 | custom fusion | bytes 3072 | tf_op jit(solution)/shard_map/jit(_take)/gather | solution.py:50
  11.5 0.1 reshape.190
  11.6 0.1 fusion.31
  11.7 0.1 and.79
  11.8 0.1 broadcast_in_dim.85
  11.9 0.1 eq.36
  12.0 0.1 copy.51
  12.1 0.1 broadcast_in_dim.86
  12.1 0.1 select_reduce_fusion
  12.3 0.7 gather_fusion.1
  13.0 3.3 %gather_fusion.2 = bf16[8,128,1024]{2,1,0:T(8,128)(2,1)} fusion(bf16[4,128,1024]{2,1,0:T(8,128)(2,1)} %param.21, s32[1024]{0:T(1024)S(1)} %pad_clamp_fusion.1), kind=kCustom, calls=%fused_computation.2.clone | custom fusion | bytes 4194336 | tf_op jit(solution)/shard_map/jit(_take)/gather | solution.py:62
  16.3 3.4 %broadcast_select_fusion = (bf16[8,128,1024]{2,1,0:T(8,128)(2,1)S(1)}, bf16[8,128,1024]{2,1,0:T(8,128)(2,1)}) fusion(bf16[8,128,1024]{2,1,0:T(8,128)(2,1)} %gather_fusion.2, pred[8]{0:T(512)(128)(4,1)S(1)} %compare_and_fusion.1, bf16[8,128,1024]{2,1,0:T(8,128)(2,1)S(1)} %gather_fusion.1), kind=kLoop, calls=%fused_computation.26 | loop fusion | flops 2097152 | bytes 8388616 | tf_op jit(solution)/shard_map/jit(_take)/select_n | solution.py:62
  19.7 37.2 %all_to_all.10 = bf16[8,128,1024]{2,1,0:T(8,128)(2,1)S(1)} all-to-all(bf16[8,128,1024]{2,1,0:T(8,128)(2,1)S(1)} %get-tuple-element.21), channel_id=1, replica_groups=mesh['region'=4,'tok'=8] {'tok'}, dimensions={0} | all-to-all | bytes 4194304 | tf_op jit(solution)/shard_map/all_to_all | solution.py:70
  56.9 4.4 %all-to-all-start = ((bf16[8,128,1024]{2,1,0:T(8,128)(2,1)}), bf16[8,128,1024]{2,1,0:T(8,128)(2,1)}, u32[]{:S(2)}, u32[]{:S(2)}) async-start(bf16[8,128,1024]{2,1,0:T(8,128)(2,1)} %get-tuple-element.22), calls=%async_computation | async-start | bytes 4194304 | tf_op jit(solution)/shard_map/all_to_all | solution.py:69
  61.3 0.0 all-gather.11.cloned.1.call-start
  61.4 0.5 all-gather.11.cloned.1.call-update
  61.9 0.1 copy.52
  62.0 0.1 compare_and_fusion
  62.1 0.6 constant_dynamic-slice_fusion.3
  65.1 0.6 dynamic_slice.32
  66.9 0.7 iota_compare_fusion.2
  67.5 0.1 broadcast_bitcast_fusion
  67.6 0.7 constant_dynamic-slice_fusion.4
  68.4 26.7 %all-to-all-done = bf16[8,128,1024]{2,1,0:T(8,128)(2,1)} async-done(((bf16[8,128,1024]{2,1,0:T(8,128)(2,1)}), bf16[8,128,1024]{2,1,0:T(8,128)(2,1)}, u32[]{:S(2)}, u32[]{:S(2)}) %all-to-all-start) | async-done | bytes 2097184 | tf_op jit(solution)/shard_map/all_to_all | solution.py:69
  95.0 1.1 constant_dynamic-slice_fusion.5
  96.1 1.8 %pad_maximum_fusion = bf16[2,128,1024]{2,1,0:T(8,128)(2,1)} fusion(bf16[1,128,1024]{2,1,0:T(8,128)(2,1)} %get-tuple-element.11, bf16[1,128,1024]{2,1,0:T(8,128)(2,1)S(1)} %get-tuple-element.9), kind=kLoop, calls=%fused_computation.39 | loop fusion | flops 262144 | bytes 1048576 | tf_op jit(solution)/shard_map/concatenate | solution.py:78
  97.9 1.5 collective-permute-start
  99.4 0.9 pad_maximum_fusion.1
  100.3 2.3 %collective-permute-start.1 = (bf16[2,128,1024]{2,1,0:T(8,128)(2,1)}, bf16[2,128,1024]{2,1,0:T(8,128)(2,1)}, u32[]{:S(2)}, u32[]{:S(2)}) collective-permute-start(bf16[2,128,1024]{2,1,0:T(8,128)(2,1)} %pad_maximum_fusion.1), channel_id=1, source_target_pairs={{8,0},{16,8},{24,16},{0,24},{9,1},{17,9},{25,17},{1,25},{10,2},{18... | collective-permute-start | bytes 1572872 | tf_op jit(solution)/shard_map/ppermute | solution.py:13
  102.6 3.5 %gather_fusion.4 = bf16[6,128,1024]{2,1,0:T(8,128)(2,1)} fusion(bf16[8,128,1024]{2,1,0:T(8,128)(2,1)} %all-to-all-done, s32[1024]{0:T(1024)S(1)} %pad_clamp_fusion), kind=kCustom, calls=%fused_computation.3.clone | custom fusion | bytes 3145752 | tf_op jit(solution)/shard_map/jit(_take)/gather | solution.py:95
  106.1 1.9 %gather_fusion.3 = bf16[6,128,1024]{2,1,0:T(8,128)(2,1)} fusion(bf16[8,128,1024]{2,1,0:T(8,128)(2,1)S(1)} %all_to_all.10, s32[1024]{0:T(1024)S(1)} %pad_clamp_fusion), kind=kCustom, calls=%fused_computation.1.clone | custom fusion | bytes 3145752 | tf_op jit(solution)/shard_map/jit(_take)/gather | solution.py:98
  107.9 2.2 %broadcast_select_fusion.3 = (bf16[6,128,1024]{2,1,0:T(8,128)(2,1)S(1)}, bf16[6,128,1024]{2,1,0:T(8,128)(2,1)S(1)}) fusion(bf16[6,128,1024]{2,1,0:T(8,128)(2,1)} %gather_fusion.3, pred[6]{0:T(512)(128)(4,1)S(1)} %get-tuple-element.6, bf16[6,128,1024]{2,1,0:T(8,128)(2,1)} %gather_fusion.4), kind=kLoop, calls=%fused_computation.29 | loop fusion | flops 1572864 | bytes 6291462 | tf_op jit(solution)/shard_map/jit(_take)/select_n | solution.py:98
  110.2 0.4 copy.69
  110.6 1.4 copy.62
  112.0 0.4 copy.66
  112.5 1.9 %copy.56 = bf16[1,768,8,128]{1,3,2,0:T(8,128)(2,1)} copy(bf16[1,768,8,128]{3,2,1,0:T(8,128)(2,1)S(1)} %bitcast.77) | data formatting | bytes 3145728 | tf_op jit(solution)/shard_map/concatenate | solution.py:106
  114.3 0.4 collective-permute-done
  114.8 1.1 fusion.35
  115.8 0.0 copy-start.2
  115.9 0.2 copy.57
  116.0 0.2 copy.60
  116.2 5.8 %collective-permute-done.1 = bf16[2,128,1024]{2,1,0:T(8,128)(2,1)} collective-permute-done((bf16[2,128,1024]{2,1,0:T(8,128)(2,1)}, bf16[2,128,1024]{2,1,0:T(8,128)(2,1)}, u32[]{:S(2)}, u32[]{:S(2)}) %collective-permute-start.1) | collective-permute-done | bytes 524320 | tf_op jit(solution)/shard_map/ppermute | solution.py:13
  122.0 1.1 fusion.36
  123.1 0.2 copy.58
  123.3 0.9 copy.61
  124.1 0.2 copy.53
  124.3 0.8 copy.54
  125.2 2.0 %fusion.21 = bf16[16,8,8,128]{3,1,2,0:T(8,128)(2,1)S(1)} fusion(bf16[128,1024]{1,0:T(8,128)(2,1)S(1)} %copy-done.2, bf16[1024,1024]{1,0:T(8,128)(2,1)} %all-gather.9.cloned.1.call-done), kind=kOutput, calls=%fused_computation.36 | convolution fusion | flops 268566528 | bytes 2621440 | tf_op jit(solution)/shard_map/dot_general | solution.py:45
  127.3 0.8 copy.59
  128.0 2.0 %convolution_convert_fusion.3 = bf16[128,1024]{1,0:T(8,128)(2,1)S(1)} fusion(bf16[128,1024]{1,0:T(8,128)(2,1)S(1)} %copy-done.2, bf16[1024,1024]{1,0:T(8,128)(2,1)} %all-gather.5.cloned.1.call-done), kind=kOutput, calls=%fused_computation.34 | convolution fusion | flops 268566528 | bytes 2621440 | tf_op jit(solution)/shard_map/dot_general | solution.py:46
  130.1 0.9 copy.64
  130.9 2.0 %fusion.20 = bf16[16,8,8,128]{3,2,1,0:T(8,128)(2,1)S(1)} fusion(bf16[128,1024]{1,0:T(8,128)(2,1)S(1)} %copy-done.2, bf16[1024,1024]{1,0:T(8,128)(2,1)} %all-gather.7.cloned.1.call-done), kind=kOutput, calls=%fused_computation.35 | convolution fusion | flops 268566528 | bytes 2621440 | tf_op jit(solution)/shard_map/dot_general | solution.py:44
  133.0 5.0 %fusion.38 = (f32[8,128]{1,0:T(8,128)S(1)}, bf16[8,128,1152]{2,1,0:T(8,128)(2,1)}) fusion(pred[1152]{0:T(1024)(128)(4,1)S(1)} %pad_reduce_fusion, bf16[1,768,8,128]{3,1,2,0:T(8,128)(2,1)} %copy.62, bf16[1,128,8,128]{3,1,2,0:T(8,128)(2,1)} %copy.61, bf16[1,128,8,128]{3,1,2,0:T(8,128)(2,1)S(1)} %copy.60, bf16[1,128,8,128]{3,1,2,0:T(8,128)(2,1)} %copy.59, ...), kind=kOutput, calls=%fused_computation.78 | convolution fusion | flops 318506112 | bytes 4985984 | tf_op jit(solution)/shard_map/sub | solution.py:124
  137.9 2.8 %fusion.25 = bf16[1,128,8,128]{1,3,2,0:T(8,128)(2,1)S(1)} fusion(bf16[8,128,1152]{2,1,0:T(8,128)(2,1)} %get-tuple-element.24, bf16[1,768,8,128]{1,3,2,0:T(8,128)(2,1)S(1)} %copy-done.3, bf16[1,128,8,128]{1,3,2,0:T(8,128)(2,1)} %bitcast.85, bf16[1,128,8,128]{1,3,2,0:T(8,128)(2,1)S(1)} %bitcast.84, bf16[1,128,8,128]{1,3,2,0:T(8,128)(2,1)} %bitcast.86, ...), kind=kOutput, calls=%fused_computation.38 | convolution fusion | flops 311689216 | bytes 4984832 | tf_op jit(solution)/shard_map/bhqk,bkhd->bqhd/dot_general | solution.py:128
  140.7 14.5 %all-gather.11.cloned.1.call-done = bf16[1024,1024]{1,0:T(8,128)(2,1)} async-done(((bf16[1024,128]{1,0:T(8,128)(2,1)}), bf16[1024,1024]{1,0:T(8,128)(2,1)}) %all-gather.11.cloned.1.call-update) | async-done | bytes 2097168 | tf_op jit(solution)/shard_map/all_gather | solution.py:133
  155.2 2.8 %convolution_convert_fusion = bf16[128,1024]{1,0:T(8,128)(2,1)} fusion(bf16[128,1024]{0,1:T(8,128)(2,1)S(1)} %bitcast.83, bf16[1024,1024]{1,0:T(8,128)(2,1)} %all-gather.11.cloned.1.call-done), kind=kOutput, calls=%fused_computation.31 | convolution fusion | flops 268566528 | bytes 2621440 | tf_op jit(solution)/shard_map/dot_general | solution.py:134
  (27 shorter events, 0.2 us)
Async XLA Ops:
  6.5 5.8 %copy-start = (bf16[4,128,1024]{2,1,0:T(8,128)(2,1)S(1)}, bf16[4,128,1024]{2,1,0:T(8,128)(2,1)}, u32[]{:S(2)}) copy-start(bf16[4,128,1024]{2,1,0:T(8,128)(2,1)} %param.20) | copy-start | bytes 3145732
  6.5 3.1 %copy-start.1 = (s32[32]{0:T(128)S(1)}, s32[32]{0:T(128)}, u32[]{:S(2)}) copy-start(s32[32]{0:T(128)} %param.25) | copy-start | bytes 388
  6.5 118.6 %all-gather.9.cloned.1.call-start = ((), (), s32[]{:S(2)}) async-start(), calls=%async_computation.4 | async-start | bytes 2359296 | tf_op jit(solution)/shard_map/all_gather | solution.py:41
  7.3 120.7 %all-gather.5.cloned.1.call-start = ((), (), s32[]{:S(2)}) async-start(), calls=%async_computation.2 | async-start | bytes 2359296 | tf_op jit(solution)/shard_map/all_gather | solution.py:42
  8.0 122.9 %all-gather.7.cloned.1.call-start = ((), (), s32[]{:S(2)}) async-start(), calls=%async_computation.3 | async-start | bytes 2359296 | tf_op jit(solution)/shard_map/all_gather | solution.py:40
  9.6 2.0 %copy-start.5 = (s32[32]{0:T(128)S(1)}, s32[32]{0:T(128)}, u32[]{:S(2)}) copy-start(s32[32]{0:T(128)} %param.24) | copy-start | bytes 388
  9.6 2.3 %copy-start.4 = (s32[32,8]{0,1:T(8,128)S(1)}, s32[32,8]{0,1:T(8,128)}, u32[]{:S(2)}) copy-start(s32[32,8]{0,1:T(8,128)} %param.23) | copy-start | bytes 3076
  56.9 38.1 %all-to-all-start = ((bf16[8,128,1024]{2,1,0:T(8,128)(2,1)}), bf16[8,128,1024]{2,1,0:T(8,128)(2,1)}, u32[]{:S(2)}, u32[]{:S(2)}) async-start(bf16[8,128,1024]{2,1,0:T(8,128)(2,1)} %get-tuple-element.22), calls=%async_computation | async-start | bytes 4194304 | tf_op jit(solution)/shard_map/all_to_all | solution.py:69
  61.3 93.9 %all-gather.11.cloned.1.call-start = ((), (), s32[]{:S(2)}) async-start(), calls=%async_computation.5 | async-start | bytes 2359296 | tf_op jit(solution)/shard_map/all_gather | solution.py:133
  97.9 16.9 %collective-permute-start = (bf16[2,128,1024]{2,1,0:T(8,128)(2,1)}, bf16[2,128,1024]{2,1,0:T(8,128)(2,1)}, u32[]{:S(2)}, u32[]{:S(2)}) collective-permute-start(bf16[2,128,1024]{2,1,0:T(8,128)(2,1)} %pad_maximum_fusion), channel_id=1, source_target_pairs={{24,0},{0,8},{8,16},{16,24},{25,1},{1,9},{9,17},{17,25},{26,2},{2,... | collective-permute-start | bytes 1572872 | tf_op jit(solution)/shard_map/ppermute | solution.py:13
  100.3 21.8 %collective-permute-start.1 = (bf16[2,128,1024]{2,1,0:T(8,128)(2,1)}, bf16[2,128,1024]{2,1,0:T(8,128)(2,1)}, u32[]{:S(2)}, u32[]{:S(2)}) collective-permute-start(bf16[2,128,1024]{2,1,0:T(8,128)(2,1)} %pad_maximum_fusion.1), channel_id=1, source_target_pairs={{8,0},{16,8},{24,16},{0,24},{9,1},{17,9},{25,17},{1,25},{10,2},{18... | collective-permute-start | bytes 1572872 | tf_op jit(solution)/shard_map/ppermute | solution.py:13
  115.8 9.3 %copy-start.2 = (bf16[128,1024]{1,0:T(8,128)(2,1)S(1)}, bf16[128,1024]{1,0:T(8,128)(2,1)}, u32[]{:S(2)}) copy-start(bf16[128,1024]{1,0:T(8,128)(2,1)} %param.15) | copy-start | bytes 786436
  133.0 5.0 %copy-start.3 = (bf16[1,768,8,128]{1,3,2,0:T(8,128)(2,1)S(1)}, bf16[1,768,8,128]{1,3,2,0:T(8,128)(2,1)}, u32[]{:S(2)}) copy-start(bf16[1,768,8,128]{1,3,2,0:T(8,128)(2,1)} %copy.56) | copy-start | bytes 4718596
Sparse Core Ops, SparseCore 0:
  9.2 41.8 all-gather.8
  53.0 40.6 all-gather.4
  95.6 29.6 all-gather.6
  127.0 28.0 all-gather.10
where the time goes:
time: 165 us; the launch traced here: 164 us
  waiting for transfers between devices  50 us (30%)
  blocking collectives  37.2 us (23%)
  local copies, waits for them, and re-layouts  26.1 us (16%)
  between operations  17 us (10%)
  matrix products  16.6 us (10%)
  other arithmetic  9.24 us (6%)
  starting transfers between devices  8.33 us (5%)
    all_to_all x1, blocking collectives, per_device(): lax.all_to_all(offer_values, 'tok', split_axis=0, concat_axis=0, tiled=True)  37.2 us
    all_to_all x1, waiting for transfers between devices, per_device(): lax.all_to_all(offer_keys, 'tok', split_axis=0, concat_axis=0, tiled=True)  26.7 us
    all_gather x1, waiting for transfers between devices, per_device(): whole_out = lax.all_gather(w_out, 'tok', axis=1, tiled=True)  14.5 us
    ppermute x2, waiting for transfers between devices, shifted(): return lax.ppermute(block, axis, route)  6.26 us
    sub x1, matrix products, per_device(): scores - row_max  4.96 us
    all_to_all x1, starting transfers between devices, per_device(): lax.all_to_all(offer_keys, 'tok', split_axis=0, concat_axis=0, tiled=True)  4.38 us
    ppermute x2, starting transfers between devices, shifted(): return lax.ppermute(block, axis, route)  3.82 us
    gather x1, local copies, waits for them, and re-layouts, per_device(): jnp.take(got_keys, own_index, axis=0)  3.47 us
  transfers between devices with their start and end apart: 7, of which 4 were waited for; matrix products, arithmetic and copies ran while one was open for 30% of the time, Pallas kernels for 0%

commit v1 on v0

--- a/solution.py
+++ b/solution.py
@@ -1,16 +1,394 @@
 import jax
 import jax.numpy as jnp
 from jax import lax
+from jax.experimental import pallas as pl
+from jax.experimental.pallas import tpu as pltpu
 from jax.sharding import PartitionSpec as P
 
 HEADS = 8
 QB = 128
+
+
+ANY = pl.BlockSpec(memory_space=pl.ANY)
+VMEM = pl.BlockSpec(memory_space=pltpu.VMEM)
+SMEM = pl.BlockSpec(memory_space=pltpu.SMEM)
 
 
 def shifted(block, axis, distance):
     devices = range(lax.axis_size(axis))
     route = [((i - distance) % len(devices), i) for i in devices]
     return lax.ppermute(block, axis, route)
+
+
+def partner(block, mask):
+    route = [(i, i ^ mask) for i in range(lax.axis_size("tok"))]
+    return lax.ppermute(block, "tok", route)
+
+
+def gathered(shard):
+    shards = [shard]
+    for mask in range(1, lax.axis_size("tok")):
+        near = mask % 2 == 1
+        shards.append(partner(shards[mask - 1] if near else shard, 1 if near else mask))
+    return shards
+
+
+def exchanged(pieces):
+    return [pieces[0]] + [partner(pieces[m], m) for m in range(1, len(pieces))]
+
+
+def swapped(pieces):
+    return lax.all_to_all(pieces, "tok", split_axis=0, concat_axis=0, tiled=True)
+
+
+def kernel(body, arguments, out_shape, in_specs, out_specs, scratch, limit, flops, moved):
+    return pl.pallas_call(
+        body,
+        out_shape=out_shape,
+        in_specs=in_specs,
+        out_specs=out_specs,
+        scratch_shapes=scratch,
+        compiler_params=pltpu.CompilerParams(vmem_limit_bytes=limit * 2**20),
+        cost_estimate=pl.CostEstimate(flops=flops, bytes_accessed=moved, transcendentals=0),
+    )(*arguments)
+
+
+def pack(sources, n_tok, mirrored):
+    width = sources[0].shape[-1]
+    head_size = width // n_tok
+    n_sources = len(sources)
+    shape = sources[0].shape[:-1] + (n_sources * head_size,)
+    dtype = sources[0].dtype
+
+    def body(*refs):
+        source_refs = refs[:n_sources]
+        out_refs = refs[n_sources:-1]
+        sems = refs[-1]
+        tok_id = lax.axis_index("tok")
+        copies = []
+        for m in range(n_tok):
+            start = m * head_size
+            if mirrored:
+                start = pl.multiple_of((tok_id ^ m) * head_size, head_size)
+            for j in range(n_sources):
+                columns = pl.ds(start, head_size)
+                source = source_refs[j]
+                view = source.at[:, :, columns] if len(shape) == 3 else source.at[:, columns]
+                target = out_refs[m] if mirrored else out_refs[0].at[m]
+                if n_sources > 1:
+                    target = target.at[:, j * head_size : (j + 1) * head_size]
+                copies.append(pltpu.make_async_copy(view, target, sems.at[m, j]))
+                copies[-1].start()
+        for copy in copies:
+            copy.wait()
+
+    if mirrored:
+        out_shape = [jax.ShapeDtypeStruct(shape, dtype)] * n_tok
+    else:
+        out_shape = jax.ShapeDtypeStruct((n_tok,) + shape, dtype)
+    return kernel(
+        body,
+        sources,
+        out_shape,
+        [ANY] * n_sources,
+        [ANY] * n_tok if mirrored else ANY,
+        [pltpu.SemaphoreType.DMA((n_tok, n_sources))],
+        4,
+        0,
+        4 * n_sources * sources[0].size,
+    )
+
+
+def pick_sides(pieces, tables, n_region, n_tok):
+    whole = not isinstance(pieces, list)
+    _, rows, head_size = pieces.shape[1:] if whole else pieces[0].shape
+    dtype = pieces.dtype if whole else pieces[0].dtype
+
+    def neighbours():
+        region_id = lax.axis_index("region")
+        upper = lax.rem(region_id + 1, n_region)
+        lower = lax.rem(region_id + n_region - 1, n_region)
+        return (0, upper), (1, lower)
+
+    def body(block_ref, frame_ref, slot_ref, *refs):
+        piece_refs = refs[: -4 if not whole else 1]
+        up_ref, down_ref, places, sems = refs[-4:]
+        tok_id = lax.axis_index("tok")
+        copies = []
+        for (entry, reader), out_ref in zip(neighbours(), (up_ref, down_ref)):
+            for m in range(n_tok):
+                query_block = reader * n_tok + (tok_id ^ m)
+                slot = slot_ref[block_ref[entry, query_block]]
+                source = lax.rem(slot, n_tok)
+                frame = frame_ref[entry, query_block]
+                if whole:
+                    copies.append(
+                        pltpu.make_async_copy(
+                            piece_refs[0].at[source, frame], out_ref.at[m], sems.at[entry, m]
+                        )
+                    )
+                    copies[-1].start()
+                else:
+                    places[0, source ^ tok_id] = m
+                    places[1, source ^ tok_id] = frame
+            if not whole:
+                for m in range(n_tok):
+                    copies.append(
+                        pltpu.make_async_copy(
+                            piece_refs[m].at[places[1, m]],
+                            out_ref.at[places[0, m]],
+                            sems.at[entry, m],
+                        )
+                    )
+                    copies[-1].start()
+        for copy in copies:
+            copy.wait()
+
+    side = jax.ShapeDtypeStruct((n_tok, rows, head_size), dtype)
+    return kernel(
+        body,
+        tables + ((pieces,) if whole else tuple(pieces)),
+        [side, side],
+        [SMEM] * 3 + [ANY] * (1 if whole else n_tok),
+        [ANY] * 2,
+        [pltpu.SMEM((2, n_tok), jnp.int32), pltpu.SemaphoreType.DMA((2, n_tok))],
+        4,
+        0,
+        8 * n_tok * rows * head_size,
+    )
+
+
+def project(token_blocks, weight_rows):
+    n_tok = len(token_blocks)
+    rows, width = token_blocks[0].shape
+    depth, columns = weight_rows[0].shape
+    dtype = token_blocks[0].dtype
+    n_chunks = 2
+    chunk = n_tok // n_chunks
+
+    def body(*refs):
+        token_refs = refs[:n_tok]
+        weight_refs = refs[n_tok : 2 * n_tok]
+        out_ref, held, whole, sems = refs[2 * n_tok :]
+        tok_id = lax.axis_index("tok")
+        weight_copies = []
+        for m in range(n_tok):
+            start = pl.multiple_of((tok_id ^ m) * depth, depth)
+            target = whole.at[pl.ds(start, depth), :]
+            weight_copies.append(pltpu.make_async_copy(weight_refs[m], target, sems.at[0, m]))
+            weight_copies[-1].start()
+        token_copies = []
+        for m in range(n_tok):
+            target = held.at[m * rows : (m + 1) * rows]
+            token_copies.append(pltpu.make_async_copy(token_refs[m], target, sems.at[1, m]))
+            token_copies[-1].start()
+        for copy in weight_copies:
+            copy.wait()
+        for c in range(n_chunks):
+            for m in range(c * chunk, (c + 1) * chunk):
+                token_copies[m].wait()
+            some = slice(c * chunk * rows, (c + 1) * chunk * rows)
+            out_ref[some] = jnp.dot(
+                held[some], whole[...], preferred_element_type=jnp.float32
+            ).astype(dtype)
+
+    out = kernel(
+        body,
+        (*token_blocks, *weight_rows),
+        jax.ShapeDtypeStruct((n_tok * rows, columns), dtype),
+        [ANY] * (2 * n_tok),
+        VMEM,
+        [
+            pltpu.VMEM((n_tok * rows, width), dtype),
+            pltpu.VMEM((n_tok * depth, columns), dtype),
+            pltpu.SemaphoreType.DMA((2, n_tok)),
+        ],
+        12,
+        2 * n_tok * rows * width * columns,
+        2 * n_tok * (rows * width + depth * columns),
+    )
+    return out.reshape(n_tok, rows, columns)
+
+
+def attend(projected, keys, values, side_keys, side_values, tables, counts):
+    n_tok, rows, columns = projected.shape
+    head_size = columns // 3
+    frames = keys.shape[1]
+    max_entries = tables[0].shape[0]
+    scale = head_size ** (-0.5)
+    across = (((1,), (1,)), ((), ()))
+
+    def body(block_ref, frame_ref, slot_ref, count_ref, proj_ref, key_ref, value_ref, *refs):
+        side_refs = refs[:4]
+        out_refs = refs[4:]
+        region_id = lax.axis_index("region")
+        tok_id = lax.axis_index("tok")
+        for m in range(n_tok):
+            query_block = region_id * n_tok + (tok_id ^ m)
+            live = count_ref[query_block]
+            query = proj_ref[m, :, :head_size]
+            key_list = [proj_ref[m, :, head_size : 2 * head_size]]
+            value_list = [proj_ref[m, :, 2 * head_size :]]
+            for entry in range(2):
+                key_list.append(side_refs[entry][m])
+                value_list.append(side_refs[2 + entry][m])
+            for entry in range(2, max_entries):
+                slot = slot_ref[block_ref[entry, query_block]]
+                source = lax.rem(slot, n_tok)
+                frame = frame_ref[entry, query_block]
+                key_list.append(key_ref[source ^ tok_id, frame])
+                value_list.append(value_ref[source, frame])
+            scores = (
+                lax.dot_general(
+                    query,
+                    jnp.concatenate(key_list, 0),
+                    across,
+                    preferred_element_type=jnp.float32,
+                )
+                * scale
+            )
+            column = lax.broadcasted_iota(jnp.int32, scores.shape, 1)
+            scores = jnp.where(column < (live + 1) * rows, scores, jnp.float32(-1e30))
+            row_max = jnp.max(scores, axis=1, keepdims=True)
+            weights = jnp.exp(scores - row_max)
+            total = jnp.sum(weights, axis=1, keepdims=True)
+            context = jnp.dot(
+                weights.astype(jnp.bfloat16),
+                jnp.concatenate(value_list, 0),
+                preferred_element_type=jnp.float32,
+            )
+            out_refs[m][...] = (context / total).astype(out_refs[m].dtype)
+
+    dtype = projected.dtype
+    return kernel(
+        body,
+        (*tables, counts, projected, keys, values, *side_keys, *side_values),
+        [jax.ShapeDtypeStruct((rows, head_size), dtype)] * n_tok,
+        [SMEM] * 4 + [VMEM] * 7,
+        [VMEM] * n_tok,
+        [],
+        16,
+        4 * n_tok * rows * rows * (max_entries + 1) * head_size,
+        4 * n_tok * frames * rows * head_size,
+    )
+
+
+def join(pieces):
+    n_pieces = len(pieces)
+    piece = pieces[0]
+
+    def body(*refs):
+        copies = [
+            pltpu.make_async_copy(refs[m], refs[n_pieces].at[m], refs[-1].at[m])
+            for m in range(n_pieces)
+        ]
+        for copy in copies:
+            copy.start()
+        for copy in copies:
+            copy.wait()
+
+    return kernel(
+        body,
+        tuple(pieces),
+        jax.ShapeDtypeStruct((n_pieces,) + piece.shape, piece.dtype),
+        [ANY] * n_pieces,
+        ANY,
+        [pltpu.SemaphoreType.DMA((n_pieces,))],
+        4,
+        0,
+        4 * n_pieces * piece.size,
+    )
+
+
+def mix(context_heads, out_columns):
+    n_tok = len(context_heads)
+    rows, head_size = context_heads[0].shape
+    width, columns = out_columns[0].shape
+    dtype = context_heads[0].dtype
+
+    def body(*refs):
+        context_refs = refs[:n_tok]
+        column_refs = refs[n_tok : 2 * n_tok]
+        out_ref, context, held, sems = refs[2 * n_tok :]
+        copies = [
+            pltpu.make_async_copy(
+                column_refs[m],
+                held.at[m // 2, :, m % 2 * columns : (m % 2 + 1) * columns],
+                sems.at[m],
+            )
+            for m in range(n_tok)
+        ]
+        for copy in copies:
+            copy.start()
+        tok_id = lax.axis_index("tok")
+        for m in range(n_tok):
+            start = pl.multiple_of((tok_id ^ m) * head_size, head_size)
+            context[:, pl.ds(start, head_size)] = context_refs[m][...]
+        for m in range(0, n_tok, 2):
+            copies[m].wait()
+            copies[m + 1].wait()
+            mixed = jnp.dot(context[...], held[m // 2], preferred_element_type=jnp.float32)
+            for j in range(2):
+                start = pl.multiple_of((tok_id ^ (m + j)) * columns, columns)
+                out_ref[:, pl.ds(start, columns)] = mixed[
+                    :, j * columns : (j + 1) * columns
+                ].astype(dtype)
+
+    return kernel(
+        body,
+        (*context_heads, *out_columns),
+        jax.ShapeDtypeStruct((rows, n_tok * columns), dtype),
+        [VMEM] * n_tok + [ANY] * n_tok,
+        VMEM,
+        [
+            pltpu.VMEM((rows, n_tok * head_size), dtype),
+            pltpu.VMEM((n_tok // 2, width, 2 * columns), dtype),
+            pltpu.SemaphoreType.DMA((n_tok,)),
+        ],
+        12,
+        2 * rows * width * n_tok * columns,
+        2 * width * n_tok * columns,
+    )
+
+
+def head_per_device(
+    tokens,
+    w_query,
+    w_key,
+    w_value,
+    w_out,
+    past_keys,
+    past_values,
+    nb_block,
+    nb_frame,
+    nb_count,
+    block_slot,
+):
+    n_region = lax.axis_size("region")
+    n_tok = lax.axis_size("tok")
+    tables = (nb_block.T, nb_frame.T, block_slot)
+    keys = exchanged(pack((past_keys,), n_tok, True))
+    values = swapped(pack((past_values,), n_tok, False))
+    up_keys, down_keys = pick_sides(keys, tables, n_region, n_tok)
+    below_keys = shifted(up_keys, "region", 1)
+    above_keys = shifted(down_keys, "region", -1)
+    up_values, down_values = pick_sides(values, tables, n_region, n_tok)
+    below_values = shifted(up_values, "region", 1)
+    above_values = shifted(down_values, "region", -1)
+    weight_rows = exchanged(pack((w_query, w_key, w_value), n_tok, True))
+    token_blocks = gathered(tokens)
+    out_columns = gathered(w_out)
+    projected = project(token_blocks, weight_rows)
+    context = attend(
+        projected,
+        join(keys),
+        values,
+        (below_keys, above_keys),
+        (below_values, above_values),
+        tables,
+        nb_count,
+    )
+    return mix(exchanged(context), out_columns)
 
 
 def per_device(
@@ -136,8 +514,9 @@
 
 
 def solution(mesh):
+    by_head = mesh.shape["tok"] == HEADS
     return jax.shard_map(
-        per_device,
+        head_per_device if by_head else per_device,
         mesh=mesh,
         in_specs=(
             P(("region", "tok"), None),

time: 165 us -> 118 us (0.72)
  blocking collectives: 37.2 us -> 0 us
  starting transfers between devices: 8.33 us -> 40.2 us
  local copies, waits for them, and re-layouts: 26.1 us -> 7.72 us
  Pallas kernels: 0 us -> 17.5 us
  between operations: 17 us -> 0.36 us
  matrix products: 16.6 us -> 0 us
  other arithmetic: 9.24 us -> 0 us
    ppermute x0 -> x35, waiting for transfers between devices: none -> 43.4 us  [partner(): return lax.ppermute(block, 'tok', route)]
    all_to_all x1 -> x0, blocking collectives: 37.2 us -> none  [per_device(): lax.all_to_all(offer_values, 'tok', split_axis=0, concat_axis=0, tiled=True)]
    ppermute x0 -> x35, starting transfers between devices: none -> 27.1 us  [partner(): return lax.ppermute(block, 'tok', route)]
    all_to_all x1, waiting for transfers between devices: 26.7 us -> 0.01 us  [swapped(): lax.all_to_all(pieces, 'tok', split_axis=0, concat_axis=0, tiled=True)]
    pallas_call x0 -> x9, Pallas kernels: none -> 17.5 us  [kernel(): pl.pallas_call(body, out_shape=out_shape, in_specs=in_specs, out_specs=ou...]
    all_gather x4 -> x0, waiting for transfers between devices: 14.5 us -> none  [the longest x1 14.5 us: per_device(): whole_out = lax.all_gather(w_out, 'tok', axis=1, tiled=True)]
    dot_general x5 -> x0, matrix products: 11.6 us -> none  [the longest x1 2.77 us: per_device(): jnp.dot(context_bf, whole_out, preferred_element_type=jnp.float32)]
    gather x6 -> x0, local copies, waits for them, and re-layouts: 11.2 us -> none  [the longest x1 3.47 us: per_device(): jnp.take(got_keys, own_index, axis=0)]
  transfers between devices with their start and end apart: 7 -> 40, of which waited for: 4 -> 9; matrix products, arithmetic and copies ran while one was open for 30% -> 0% of each run, Pallas kernels for 0% -> 12%
where the time goes in v1:
time: 118 us; the launch traced here: 117 us
  waiting for transfers between devices  50.9 us (43%)
  starting transfers between devices  40.2 us (34%)
  Pallas kernels  17.5 us (15%)
  local copies, waits for them, and re-layouts  7.72 us (7%)
    ppermute x35, waiting for transfers between devices, partner(): return lax.ppermute(block, 'tok', route)  43.4 us
    ppermute x35, starting transfers between devices, partner(): return lax.ppermute(block, 'tok', route)  27.1 us
    pallas_call x9, Pallas kernels, kernel(): pl.pallas_call(body, out_shape=out_shape, in_specs=in_specs, out_specs=ou...  17.5 us
    ppermute x4, starting transfers between devices, shifted(): return lax.ppermute(block, axis, route)  7.78 us
    unnamed x60, local copies, waits for them, and re-layouts  7.72 us
    ppermute x4, waiting for transfers between devices, shifted(): return lax.ppermute(block, axis, route)  7.49 us
    all_to_all x1, starting transfers between devices, swapped(): lax.all_to_all(pieces, 'tok', split_axis=0, concat_axis=0, tiled=True)  5.34 us
  transfers between devices with their start and end apart: 40, of which 9 were waited for; matrix products, arithmetic and copies ran while one was open for 0% of the time, Pallas kernels for 12%

profile of v1, /device:TPU:0, one launch (start us, length us, event | category | flops | bytes accessed | tf_op | source)
XLA Modules:
  0.0 116.7 jit_solution(10522258679316194318)
XLA Ops:
  0.0 1.2 %copy-done = bf16[4,128,1024]{2,1,0:T(8,128)(2,1)S(1)} copy-done((bf16[4,128,1024]{2,1,0:T(8,128)(2,1)S(1)}, bf16[4,128,1024]{2,1,0:T(8,128)(2,1)}, u32[]{:S(2)}) %copy-start) | copy-done | bytes 1048600
  1.2 1.1 shard_map.113
  2.3 0.0 copy-start.3
  2.4 5.3 %all-to-all-start = ((bf16[8,4,128,128]{3,2,1,0:T(8,128)(2,1)}), bf16[8,4,128,128]{3,2,1,0:T(8,128)(2,1)S(1)}, u32[]{:S(2)}, u32[]{:S(2)}) async-start(bf16[8,4,128,128]{3,2,1,0:T(8,128)(2,1)} %shard_map.113), calls=%async_computation | async-start | bytes 2097152 | tf_op jit(solution)/shard_map/all_to_all | solution.py:41
  7.7 0.5 shard_map.109
  8.2 2.1 %collective-permute-start.10 = (bf16[128,384]{1,0:T(8,128)(2,1)S(1)}, bf16[128,384]{1,0:T(8,128)(2,1)S(1)}, u32[]{:S(2)}, u32[]{:S(2)}) collective-permute-start(bf16[128,384]{1,0:T(8,128)(2,1)S(1)} %get-tuple-element.37), channel_id=1, source_target_pairs={{0,4},{1,5},{2,6},{3,7},{4,0},{5,1},{6,2},{7,3},{8,12},{9,13},{10,... | collective-permute-start | bytes 294920 | tf_op jit(solution)/shard_map/ppermute | solution.py:25
  10.3 2.4 %collective-permute-start.12 = (bf16[128,384]{1,0:T(8,128)(2,1)S(1)}, bf16[128,384]{1,0:T(8,128)(2,1)S(1)}, u32[]{:S(2)}, u32[]{:S(2)}) collective-permute-start(bf16[128,384]{1,0:T(8,128)(2,1)S(1)} %get-tuple-element.39), channel_id=1, source_target_pairs={{0,6},{1,7},{2,4},{3,5},{4,2},{5,3},{6,0},{7,1},{8,14},{9,15},{10,... | collective-permute-start | bytes 294920 | tf_op jit(solution)/shard_map/ppermute | solution.py:25
  12.7 0.3 collective-permute-start.13
  13.0 0.4 collective-permute-start.7
  13.4 15.6 %collective-permute-done.10.refs_12_ = bf16[128,384]{1,0:T(8,128)(2,1)S(1)} collective-permute-done((bf16[128,384]{1,0:T(8,128)(2,1)S(1)}, bf16[128,384]{1,0:T(8,128)(2,1)S(1)}, u32[]{:S(2)}, u32[]{:S(2)}) %collective-permute-start.10) | collective-permute-done | bytes 98336 | tf_op jit(solution)/shard_map/ppermute | solution.py:25
  29.0 0.6 copy-done.12
  29.7 0.9 collective-permute-start.8
  30.6 0.4 shard_map.111
  31.0 0.6 copy-done.14
  31.6 0.6 copy-done.16
  32.3 1.1 collective-permute-start.15
  33.4 0.6 copy-done.18
  34.0 0.8 collective-permute-start.16
  34.8 0.6 copy-done.20
  35.4 1.0 collective-permute-start.9
  36.4 0.6 copy-done.22
  37.0 0.4 collective-permute-start.17
  37.4 5.2 %collective-permute-done.9.refs_11_ = bf16[128,384]{1,0:T(8,128)(2,1)S(1)} collective-permute-done((bf16[128,384]{1,0:T(8,128)(2,1)S(1)}, bf16[128,384]{1,0:T(8,128)(2,1)S(1)}, u32[]{:S(2)}, u32[]{:S(2)}) %collective-permute-start.9) | collective-permute-done | bytes 98336 | tf_op jit(solution)/shard_map/ppermute | solution.py:25
  42.6 0.6 copy-done.24
  43.3 0.3 collective-permute-start.18
  43.6 1.0 collective-permute-start.1
  44.5 1.8 %collective-permute-start.3 = (bf16[128,1024]{1,0:T(8,128)(2,1)S(1)}, bf16[128,1024]{1,0:T(8,128)(2,1)S(1)}, u32[]{:S(2)}, u32[]{:S(2)}) collective-permute-start(bf16[128,1024]{1,0:T(8,128)(2,1)S(1)} %copy-done.2), channel_id=1, source_target_pairs={{0,4},{1,5},{2,6},{3,7},{4,0},{5,1},{6,2},{7,3},{8,12},{9,13},{10,... | collective-permute-start | bytes 786440 | tf_op jit(solution)/shard_map/ppermute | solution.py:25
  46.3 0.8 collective-permute-start.5
  47.1 2.2 %collective-permute-start.19 = (bf16[4,128,128]{2,1,0:T(8,128)(2,1)S(1)}, bf16[4,128,128]{2,1,0:T(8,128)(2,1)S(1)}, u32[]{:S(2)}, u32[]{:S(2)}) collective-permute-start(bf16[4,128,128]{2,1,0:T(8,128)(2,1)S(1)} %get-tuple-element.47), channel_id=1, source_target_pairs={{0,6},{1,7},{2,4},{3,5},{4,2},{5,3},{6,0},{7,1},{8,14},{9,15},{10,... | collective-permute-start | bytes 393224 | tf_op jit(solution)/shard_map/ppermute | solution.py:25
  49.2 0.8 collective-permute-start.20
  50.0 12.3 %collective-permute-done.19.refs_6_ = bf16[4,128,128]{2,1,0:T(8,128)(2,1)S(1)} collective-permute-done((bf16[4,128,128]{2,1,0:T(8,128)(2,1)S(1)}, bf16[4,128,128]{2,1,0:T(8,128)(2,1)S(1)}, u32[]{:S(2)}, u32[]{:S(2)}) %collective-permute-start.19) | collective-permute-done | bytes 131104 | tf_op jit(solution)/shard_map/ppermute | solution.py:25
  62.3 1.3 %collective-permute-done.20.refs_7_ = bf16[4,128,128]{2,1,0:T(8,128)(2,1)S(1)} collective-permute-done((bf16[4,128,128]{2,1,0:T(8,128)(2,1)S(1)}, bf16[4,128,128]{2,1,0:T(8,128)(2,1)S(1)}, u32[]{:S(2)}, u32[]{:S(2)}) %collective-permute-start.20) | collective-permute-done | bytes 131104 | tf_op jit(solution)/shard_map/ppermute | solution.py:25
  63.7 1.1 collective-permute-start.33
  64.7 0.2 collective-permute-start.35
  65.0 0.6 copy-done.28
  65.6 1.6 %shard_map.114 = (bf16[8,128,128]{2,1,0:T(8,128)(2,1)}, bf16[8,128,128]{2,1,0:T(8,128)(2,1)}) custom-call(s32[8,32]{1,0:T(8,128)S(1)} %bitcast.4, s32[8,32]{1,0:T(8,128)S(1)} %bitcast.7, s32[32]{0:T(128)S(1)} %copy-done.28, bf16[4,128,128]{2,1,0:T(8,128)(2,1)S(1)} %get-tuple-element.41.refs_0_, bf16[4,128,128]{2,1,0:T(8,128)(2,1)S(1)} %collective-permute-done.14.refs_1_, ...), custom_call_target="tpu_custom_call" | custom-call | bytes 1048576 | tf_op jit(solution)/shard_map/pallas_call | solution.py:45
  67.3 2.2 %collective-permute-start.37 = (bf16[1024,128]{1,0:T(8,128)(2,1)}, bf16[1024,128]{1,0:T(8,128)(2,1)}, u32[]{:S(2)}, u32[]{:S(2)}) collective-permute-start(bf16[1024,128]{1,0:T(8,128)(2,1)} %refs_8_.1), channel_id=1, source_target_pairs={{0,6},{1,7},{2,4},{3,5},{4,2},{5,3},{6,0},{7,1},{8,14},{9,15},{10,... | collective-permute-start | bytes 786440 | tf_op jit(solution)/shard_map/ppermute | solution.py:25
  69.5 1.6 %collective-permute-start.21 = (bf16[8,128,128]{2,1,0:T(8,128)(2,1)}, bf16[8,128,128]{2,1,0:T(8,128)(2,1)}, u32[]{:S(2)}, u32[]{:S(2)}) collective-permute-start(bf16[8,128,128]{2,1,0:T(8,128)(2,1)} %get-tuple-element.49), channel_id=1, source_target_pairs={{24,0},{0,8},{8,16},{16,24},{25,1},{1,9},{9,17},{17,25},{26,2},{2,... | collective-permute-start | bytes 786440 | tf_op jit(solution)/shard_map/ppermute | solution.py:20
  71.1 2.2 %collective-permute-start.22 = (bf16[8,128,128]{2,1,0:T(8,128)(2,1)}, bf16[8,128,128]{2,1,0:T(8,128)(2,1)}, u32[]{:S(2)}, u32[]{:S(2)}) collective-permute-start(bf16[8,128,128]{2,1,0:T(8,128)(2,1)} %get-tuple-element.50), channel_id=1, source_target_pairs={{8,0},{16,8},{24,16},{0,24},{9,1},{17,9},{25,17},{1,25},{10,2},{18... | collective-permute-start | bytes 786440 | tf_op jit(solution)/shard_map/ppermute | solution.py:20
  73.4 5.7 %collective-permute-done.35.refs_12_ = bf16[1024,128]{1,0:T(8,128)(2,1)S(1)} collective-permute-done((bf16[1024,128]{1,0:T(8,128)(2,1)}, bf16[1024,128]{1,0:T(8,128)(2,1)S(1)}, u32[]{:S(2)}, u32[]{:S(2)}) %collective-permute-start.35) | collective-permute-done | bytes 262176 | tf_op jit(solution)/shard_map/ppermute | solution.py:25
  79.1 0.7 copy-done.8
  79.8 1.7 %shard_map.115 = (bf16[8,128,128]{2,1,0:T(8,128)(2,1)S(1)}, bf16[8,128,128]{2,1,0:T(8,128)(2,1)S(1)}) custom-call(s32[8,32]{1,0:T(8,128)S(1)} %bitcast.5, s32[8,32]{1,0:T(8,128)S(1)} %bitcast.8, s32[32]{0:T(128)S(1)} %copy-done.28, bf16[8,4,128,128]{3,2,1,0:T(8,128)(2,1)S(1)} %all-to-all-done.refs_0_.value_ref), custom_call_target="tpu_custom_call" | custom-call | bytes 1048576 | tf_op jit(solution)/shard_map/pallas_call | solution.py:45
  81.5 0.6 collective-permute-start.6
  82.1 1.6 %collective-permute-start.23 = (bf16[8,128,128]{2,1,0:T(8,128)(2,1)S(1)}, bf16[8,128,128]{2,1,0:T(8,128)(2,1)S(1)}, u32[]{:S(2)}, u32[]{:S(2)}) collective-permute-start(bf16[8,128,128]{2,1,0:T(8,128)(2,1)S(1)} %get-tuple-element.51), channel_id=1, source_target_pairs={{24,0},{0,8},{8,16},{16,24},{25,1},{1,9},{9,17},{17,25},{26,2},{2,... | collective-permute-start | bytes 786440 | tf_op jit(solution)/shard_map/ppermute | solution.py:20
  83.7 1.0 collective-permute-done.22.refs_1_
  84.8 2.4 %collective-permute-start.24 = (bf16[8,128,128]{2,1,0:T(8,128)(2,1)S(1)}, bf16[8,128,128]{2,1,0:T(8,128)(2,1)S(1)}, u32[]{:S(2)}, u32[]{:S(2)}) collective-permute-start(bf16[8,128,128]{2,1,0:T(8,128)(2,1)S(1)} %get-tuple-element.52), channel_id=1, source_target_pairs={{8,0},{16,8},{24,16},{0,24},{9,1},{17,9},{25,17},{1,25},{10,2},{18... | collective-permute-start | bytes 786440 | tf_op jit(solution)/shard_map/ppermute | solution.py:20
  87.2 0.5 collective-permute-start.34
  87.7 0.1 collective-permute-start.36
  87.8 6.5 %collective-permute-done.23.refs_2_ = bf16[8,128,128]{2,1,0:T(8,128)(2,1)S(1)} collective-permute-done((bf16[8,128,128]{2,1,0:T(8,128)(2,1)S(1)}, bf16[8,128,128]{2,1,0:T(8,128)(2,1)S(1)}, u32[]{:S(2)}, u32[]{:S(2)}) %collective-permute-start.23) | collective-permute-done | bytes 262176 | tf_op jit(solution)/shard_map/ppermute | solution.py:20
  94.2 1.4 %shard_map.112.key_ref = bf16[8,4,128,128]{3,2,1,0:T(8,128)(2,1)S(1)} custom-call(bf16[4,128,128]{2,1,0:T(8,128)(2,1)S(1)} %get-tuple-element.41.refs_0_, bf16[4,128,128]{2,1,0:T(8,128)(2,1)S(1)} %collective-permute-done.14.refs_1_, bf16[4,128,128]{2,1,0:T(8,128)(2,1)S(1)} %collective-permute-done.15.refs_2_, ...), custom_call_target="tpu_custom_call" | custom-call | bytes 2097152 | tf_op jit(solution)/shard_map/pallas_call | solution.py:45
  95.7 3.6 %shard_map.110 = bf16[1024,384]{1,0:T(8,128)(2,1)S(1)} custom-call(bf16[128,1024]{1,0:T(8,128)(2,1)S(1)} %copy-done.2, bf16[128,1024]{1,0:T(8,128)(2,1)S(1)} %collective-permute-done.refs_1_, bf16[128,1024]{1,0:T(8,128)(2,1)S(1)} %collective-permute-done.1.refs_2_, bf16[128,1024]{1,0:T(8,128)(2,1)} %collective-permute-done.2.refs_3_, ...), custom_call_target="tpu_custom_call" | custom-call | flops 805306368 | bytes 2883584 | tf_op jit(solution)/shard_map/pallas_call | solution.py:45
  99.4 0.6 copy-done.29
  100.0 4.3 %shard_map.116 = (bf16[128,128]{1,0:T(8,128)(2,1)S(1)}, bf16[128,128]{1,0:T(8,128)(2,1)S(1)}, bf16[128,128]{1,0:T(8,128)(2,1)S(1)}, bf16[128,128]{1,0:T(8,128)(2...) custom-call(s32[8,32]{1,0:T(8,128)S(1)} %bitcast.6, ...), custom_call_target="tpu_custom_call" | custom-call | flops 603979776 | bytes 2097152 | tf_op jit(solution)/shard_map/pallas_call | solution.py:45
  104.3 0.6 collective-permute-start.25
  104.8 1.1 collective-permute-start.26
  105.9 0.4 collective-permute-start.27
  106.3 0.3 collective-permute-start.28
  106.6 1.7 %collective-permute-start.29 = (bf16[128,128]{1,0:T(8,128)(2,1)S(1)}, bf16[128,128]{1,0:T(8,128)(2,1)S(1)}, u32[]{:S(2)}, u32[]{:S(2)}) collective-permute-start(bf16[128,128]{1,0:T(8,128)(2,1)S(1)} %get-tuple-element.58), channel_id=1, source_target_pairs={{0,5},{1,4},{2,7},{3,6},{4,1},{5,0},{6,3},{7,2},{8,13},{9,12},{10,... | collective-permute-start | bytes 98312 | tf_op jit(solution)/shard_map/ppermute | solution.py:25
  108.3 0.9 collective-permute-start.30
  109.2 1.5 %collective-permute-start.31 = (bf16[128,128]{1,0:T(8,128)(2,1)S(1)}, bf16[128,128]{1,0:T(8,128)(2,1)S(1)}, u32[]{:S(2)}, u32[]{:S(2)}) collective-permute-start(bf16[128,128]{1,0:T(8,128)(2,1)S(1)} %get-tuple-element.60), channel_id=1, source_target_pairs={{0,7},{1,6},{2,5},{3,4},{4,3},{5,2},{6,1},{7,0},{8,15},{9,14},{10,... | collective-permute-start | bytes 98312 | tf_op jit(solution)/shard_map/ppermute | solution.py:25
  110.7 0.0 collective-permute-done.29.refs_5_
  110.7 2.5 %collective-permute-done.30.refs_6_ = bf16[128,128]{1,0:T(8,128)(2,1)S(1)} collective-permute-done((bf16[128,128]{1,0:T(8,128)(2,1)S(1)}, bf16[128,128]{1,0:T(8,128)(2,1)S(1)}, u32[]{:S(2)}, u32[]{:S(2)}) %collective-permute-start.30) | collective-permute-done | bytes 32800 | tf_op jit(solution)/shard_map/ppermute | solution.py:25
  113.2 0.6 collective-permute-done.31.refs_7_
  113.8 2.9 %shard_map.117 = bf16[128,1024]{1,0:T(8,128)(2,1)} custom-call(bf16[128,128]{1,0:T(8,128)(2,1)S(1)} %get-tuple-element.53.refs_0_, bf16[128,128]{1,0:T(8,128)(2,1)S(1)} %collective-permute-done.25.refs_1_, bf16[128,128]{1,0:T(8,128)(2,1)S(1)} %collective-permute-done.26.refs_2_, bf16[128,128]{1,0:T(8,128)(2,1)S(1)} %collective-permute-done.27.refs_3_, ...), custom_call_target="tpu_custom_call" | custom-call | flops 268435456 | bytes 2097152 | tf_op jit(solution)/shard_map/pallas_call | solution.py:45
  (85 shorter events, 0.2 us)
Async XLA Ops:
  0.0 1.2 %copy-start = (bf16[4,128,1024]{2,1,0:T(8,128)(2,1)S(1)}, bf16[4,128,1024]{2,1,0:T(8,128)(2,1)}, u32[]{:S(2)}) copy-start(bf16[4,128,1024]{2,1,0:T(8,128)(2,1)} %refs_0_.7) | copy-start | bytes 3145732
  2.3 5.4 %copy-start.3 = (bf16[128,1024]{1,0:T(8,128)(2,1)S(1)}, bf16[128,1024]{1,0:T(8,128)(2,1)}, u32[]{:S(2)}) copy-start(bf16[128,1024]{1,0:T(8,128)(2,1)} %refs_0_.4) | copy-start | bytes 786436
  2.3 5.4 %copy-start.4 = (bf16[128,1024]{1,0:T(8,128)(2,1)S(1)}, bf16[128,1024]{1,0:T(8,128)(2,1)}, u32[]{:S(2)}) copy-start(bf16[128,1024]{1,0:T(8,128)(2,1)} %refs_1_.1) | copy-start | bytes 786436
  2.3 5.4 %copy-start.5 = (bf16[128,1024]{1,0:T(8,128)(2,1)S(1)}, bf16[128,1024]{1,0:T(8,128)(2,1)}, u32[]{:S(2)}) copy-start(bf16[128,1024]{1,0:T(8,128)(2,1)} %refs_2_.1) | copy-start | bytes 786436
  2.3 28.3 %copy-start.1 = (bf16[4,128,1024]{2,1,0:T(8,128)(2,1)S(1)}, bf16[4,128,1024]{2,1,0:T(8,128)(2,1)}, u32[]{:S(2)}) copy-start(bf16[4,128,1024]{2,1,0:T(8,128)(2,1)} %refs_0_.6) | copy-start | bytes 3145732
  2.4 77.4 %all-to-all-start = ((bf16[8,4,128,128]{3,2,1,0:T(8,128)(2,1)}), bf16[8,4,128,128]{3,2,1,0:T(8,128)(2,1)S(1)}, u32[]{:S(2)}, u32[]{:S(2)}) async-start(bf16[8,4,128,128]{3,2,1,0:T(8,128)(2,1)} %shard_map.113), calls=%async_computation | async-start | bytes 2097152 | tf_op jit(solution)/shard_map/all_to_all | solution.py:41
  8.2 22.7 %copy-start.10 = (bf16[128,384]{1,0:T(8,128)(2,1)}, bf16[128,384]{1,0:T(8,128)(2,1)S(1)}, u32[]{:S(2)}) copy-start(bf16[128,384]{1,0:T(8,128)(2,1)S(1)} %get-tuple-element.33.refs_8_) | copy-start | bytes 294916
  8.2 20.8 %collective-permute-start.10 = (bf16[128,384]{1,0:T(8,128)(2,1)S(1)}, bf16[128,384]{1,0:T(8,128)(2,1)S(1)}, u32[]{:S(2)}, u32[]{:S(2)}) collective-permute-start(bf16[128,384]{1,0:T(8,128)(2,1)S(1)} %get-tuple-element.37), channel_id=1, source_target_pairs={{0,4},{1,5},{2,6},{3,7},{4,0},{5,1},{6,2},{7,3},{8,12},{9,13},{10,... | collective-permute-start | bytes 294920 | tf_op jit(solution)/shard_map/ppermute | solution.py:25
  10.3 20.7 %collective-permute-start.11 = (bf16[128,384]{1,0:T(8,128)(2,1)S(1)}, bf16[128,384]{1,0:T(8,128)(2,1)S(1)}, u32[]{:S(2)}, u32[]{:S(2)}) collective-permute-start(bf16[128,384]{1,0:T(8,128)(2,1)S(1)} %get-tuple-element.38), channel_id=1, source_target_pairs={{0,5},{1,4},{2,7},{3,6},{4,1},{5,0},{6,3},{7,2},{8,13},{9,12},{10,... | collective-permute-start | bytes 294920 | tf_op jit(solution)/shard_map/ppermute | solution.py:25
  10.3 21.3 %collective-permute-start.12 = (bf16[128,384]{1,0:T(8,128)(2,1)S(1)}, bf16[128,384]{1,0:T(8,128)(2,1)S(1)}, u32[]{:S(2)}, u32[]{:S(2)}) collective-permute-start(bf16[128,384]{1,0:T(8,128)(2,1)S(1)} %get-tuple-element.39), channel_id=1, source_target_pairs={{0,6},{1,7},{2,4},{3,5},{4,2},{5,3},{6,0},{7,1},{8,14},{9,15},{10,... | collective-permute-start | bytes 294920 | tf_op jit(solution)/shard_map/ppermute | solution.py:25
  12.7 20.7 %collective-permute-start.13 = (bf16[128,384]{1,0:T(8,128)(2,1)S(1)}, bf16[128,384]{1,0:T(8,128)(2,1)S(1)}, u32[]{:S(2)}, u32[]{:S(2)}) collective-permute-start(bf16[128,384]{1,0:T(8,128)(2,1)S(1)} %get-tuple-element.40), channel_id=1, source_target_pairs={{0,7},{1,6},{2,5},{3,4},{4,3},{5,2},{6,1},{7,0},{8,15},{9,14},{10,... | collective-permute-start | bytes 294920 | tf_op jit(solution)/shard_map/ppermute | solution.py:25
  13.0 21.8 %collective-permute-start.7 = (bf16[128,384]{1,0:T(8,128)(2,1)S(1)}, bf16[128,384]{1,0:T(8,128)(2,1)S(1)}, u32[]{:S(2)}, u32[]{:S(2)}) collective-permute-start(bf16[128,384]{1,0:T(8,128)(2,1)S(1)} %get-tuple-element.34), channel_id=1, source_target_pairs={{0,1},{1,0},{2,3},{3,2},{4,5},{5,4},{6,7},{7,6},{8,9},{9,8},{10,11... | collective-permute-start | bytes 294920 | tf_op jit(solution)/shard_map/ppermute | solution.py:25
  29.7 13.9 %copy-start.2 = (bf16[128,1024]{1,0:T(8,128)(2,1)S(1)}, bf16[128,1024]{1,0:T(8,128)(2,1)}, u32[]{:S(2)}) copy-start(bf16[128,1024]{1,0:T(8,128)(2,1)} %refs_0_.5) | copy-start | bytes 786436
  29.7 6.7 %collective-permute-start.8 = (bf16[128,384]{1,0:T(8,128)(2,1)S(1)}, bf16[128,384]{1,0:T(8,128)(2,1)S(1)}, u32[]{:S(2)}, u32[]{:S(2)}) collective-permute-start(bf16[128,384]{1,0:T(8,128)(2,1)S(1)} %get-tuple-element.35), channel_id=1, source_target_pairs={{0,2},{1,3},{2,0},{3,1},{4,6},{5,7},{6,4},{7,5},{8,10},{9,11},{10,... | collective-permute-start | bytes 294920 | tf_op jit(solution)/shard_map/ppermute | solution.py:25
  31.6 11.9 %collective-permute-start.14 = (bf16[4,128,128]{2,1,0:T(8,128)(2,1)S(1)}, bf16[4,128,128]{2,1,0:T(8,128)(2,1)S(1)}, u32[]{:S(2)}, u32[]{:S(2)}) collective-permute-start(bf16[4,128,128]{2,1,0:T(8,128)(2,1)S(1)} %get-tuple-element.42), channel_id=1, source_target_pairs={{0,1},{1,0},{2,3},{3,2},{4,5},{5,4},{6,7},{7,6},{8,9},{9,8},{10,11... | collective-permute-start | bytes 393224 | tf_op jit(solution)/shard_map/ppermute | solution.py:25
  32.3 12.3 %collective-permute-start.15 = (bf16[4,128,128]{2,1,0:T(8,128)(2,1)S(1)}, bf16[4,128,128]{2,1,0:T(8,128)(2,1)S(1)}, u32[]{:S(2)}, u32[]{:S(2)}) collective-permute-start(bf16[4,128,128]{2,1,0:T(8,128)(2,1)S(1)} %get-tuple-element.43), channel_id=1, source_target_pairs={{0,2},{1,3},{2,0},{3,1},{4,6},{5,7},{6,4},{7,5},{8,10},{9,11},{10,... | collective-permute-start | bytes 393224 | tf_op jit(solution)/shard_map/ppermute | solution.py:25
  34.0 12.3 %collective-permute-start.16 = (bf16[4,128,128]{2,1,0:T(8,128)(2,1)S(1)}, bf16[4,128,128]{2,1,0:T(8,128)(2,1)S(1)}, u32[]{:S(2)}, u32[]{:S(2)}) collective-permute-start(bf16[4,128,128]{2,1,0:T(8,128)(2,1)S(1)} %get-tuple-element.44), channel_id=1, source_target_pairs={{0,3},{1,2},{2,1},{3,0},{4,7},{5,6},{6,5},{7,4},{8,11},{9,10},{10,... | collective-permute-start | bytes 393224 | tf_op jit(solution)/shard_map/ppermute | solution.py:25
  34.8 0.6 copy-start.20
  35.4 7.2 %collective-permute-start.9 = (bf16[128,384]{1,0:T(8,128)(2,1)S(1)}, bf16[128,384]{1,0:T(8,128)(2,1)S(1)}, u32[]{:S(2)}, u32[]{:S(2)}) collective-permute-start(bf16[128,384]{1,0:T(8,128)(2,1)S(1)} %get-tuple-element.36), channel_id=1, source_target_pairs={{0,3},{1,2},{2,1},{3,0},{4,7},{5,6},{6,5},{7,4},{8,11},{9,10},{10,... | collective-permute-start | bytes 294920 | tf_op jit(solution)/shard_map/ppermute | solution.py:25
  37.0 10.0 %collective-permute-start.17 = (bf16[4,128,128]{2,1,0:T(8,128)(2,1)S(1)}, bf16[4,128,128]{2,1,0:T(8,128)(2,1)S(1)}, u32[]{:S(2)}, u32[]{:S(2)}) collective-permute-start(bf16[4,128,128]{2,1,0:T(8,128)(2,1)S(1)} %get-tuple-element.45), channel_id=1, source_target_pairs={{0,4},{1,5},{2,6},{3,7},{4,0},{5,1},{6,2},{7,3},{8,12},{9,13},{10,... | collective-permute-start | bytes 393224 | tf_op jit(solution)/shard_map/ppermute | solution.py:25
  43.3 6.0 %collective-permute-start.18 = (bf16[4,128,128]{2,1,0:T(8,128)(2,1)S(1)}, bf16[4,128,128]{2,1,0:T(8,128)(2,1)S(1)}, u32[]{:S(2)}, u32[]{:S(2)}) collective-permute-start(bf16[4,128,128]{2,1,0:T(8,128)(2,1)S(1)} %get-tuple-element.46), channel_id=1, source_target_pairs={{0,5},{1,4},{2,7},{3,6},{4,1},{5,0},{6,3},{7,2},{8,13},{9,12},{10,... | collective-permute-start | bytes 393224 | tf_op jit(solution)/shard_map/ppermute | solution.py:25
  43.6 21.2 %collective-permute-start.1 = (bf16[128,1024]{1,0:T(8,128)(2,1)S(1)}, bf16[128,1024]{1,0:T(8,128)(2,1)S(1)}, u32[]{:S(2)}, u32[]{:S(2)}) collective-permute-start(bf16[128,1024]{1,0:T(8,128)(2,1)S(1)} %copy-done.2), channel_id=1, source_target_pairs={{0,2},{1,3},{2,0},{3,1},{4,6},{5,7},{6,4},{7,5},{8,10},{9,11},{10,... | collective-permute-start | bytes 786440 | tf_op jit(solution)/shard_map/ppermute | solution.py:25
  44.5 22.7 %collective-permute-start.3 = (bf16[128,1024]{1,0:T(8,128)(2,1)S(1)}, bf16[128,1024]{1,0:T(8,128)(2,1)S(1)}, u32[]{:S(2)}, u32[]{:S(2)}) collective-permute-start(bf16[128,1024]{1,0:T(8,128)(2,1)S(1)} %copy-done.2), channel_id=1, source_target_pairs={{0,4},{1,5},{2,6},{3,7},{4,0},{5,1},{6,2},{7,3},{8,12},{9,13},{10,... | collective-permute-start | bytes 786440 | tf_op jit(solution)/shard_map/ppermute | solution.py:25
  46.3 23.2 %collective-permute-start.5 = (bf16[128,1024]{1,0:T(8,128)(2,1)S(1)}, bf16[128,1024]{1,0:T(8,128)(2,1)S(1)}, u32[]{:S(2)}, u32[]{:S(2)}) collective-permute-start(bf16[128,1024]{1,0:T(8,128)(2,1)S(1)} %copy-done.2), channel_id=1, source_target_pairs={{0,6},{1,7},{2,4},{3,5},{4,2},{5,3},{6,0},{7,1},{8,14},{9,15},{10,... | collective-permute-start | bytes 786440 | tf_op jit(solution)/shard_map/ppermute | solution.py:25
  47.1 17.9 %copy-start.27 = (s32[32,8]{0,1:T(8,128)S(1)}, s32[32,8]{0,1:T(8,128)}, u32[]{:S(2)}) copy-start(s32[32,8]{0,1:T(8,128)} %param.19) | copy-start | bytes 3076
  47.1 17.9 %copy-start.26 = (s32[32,8]{0,1:T(8,128)S(1)}, s32[32,8]{0,1:T(8,128)}, u32[]{:S(2)}) copy-start(s32[32,8]{0,1:T(8,128)} %param.18) | copy-start | bytes 3076
  47.1 15.3 %collective-permute-start.19 = (bf16[4,128,128]{2,1,0:T(8,128)(2,1)S(1)}, bf16[4,128,128]{2,1,0:T(8,128)(2,1)S(1)}, u32[]{:S(2)}, u32[]{:S(2)}) collective-permute-start(bf16[4,128,128]{2,1,0:T(8,128)(2,1)S(1)} %get-tuple-element.47), channel_id=1, source_target_pairs={{0,6},{1,7},{2,4},{3,5},{4,2},{5,3},{6,0},{7,1},{8,14},{9,15},{10,... | collective-permute-start | bytes 393224 | tf_op jit(solution)/shard_map/ppermute | solution.py:25
  49.2 14.4 %collective-permute-start.20 = (bf16[4,128,128]{2,1,0:T(8,128)(2,1)S(1)}, bf16[4,128,128]{2,1,0:T(8,128)(2,1)S(1)}, u32[]{:S(2)}, u32[]{:S(2)}) collective-permute-start(bf16[4,128,128]{2,1,0:T(8,128)(2,1)S(1)} %get-tuple-element.48), channel_id=1, source_target_pairs={{0,7},{1,6},{2,5},{3,4},{4,3},{5,2},{6,1},{7,0},{8,15},{9,14},{10,... | collective-permute-start | bytes 393224 | tf_op jit(solution)/shard_map/ppermute | solution.py:25
  62.3 8.8 %collective-permute-start = (bf16[128,1024]{1,0:T(8,128)(2,1)S(1)}, bf16[128,1024]{1,0:T(8,128)(2,1)S(1)}, u32[]{:S(2)}, u32[]{:S(2)}) collective-permute-start(bf16[128,1024]{1,0:T(8,128)(2,1)S(1)} %copy-done.2), channel_id=1, source_target_pairs={{0,1},{1,0},{2,3},{3,2},{4,5},{5,4},{6,7},{7,6},{8,9},{9,8},{10,11... | collective-permute-start | bytes 786440 | tf_op jit(solution)/shard_map/ppermute | solution.py:25
  63.7 9.7 %collective-permute-start.33 = (bf16[1024,128]{1,0:T(8,128)(2,1)}, bf16[1024,128]{1,0:T(8,128)(2,1)S(1)}, u32[]{:S(2)}, u32[]{:S(2)}) collective-permute-start(bf16[1024,128]{1,0:T(8,128)(2,1)} %refs_8_.1), channel_id=1, source_target_pairs={{0,2},{1,3},{2,0},{3,1},{4,6},{5,7},{6,4},{7,5},{8,10},{9,11},{10,... | collective-permute-start | bytes 786440 | tf_op jit(solution)/shard_map/ppermute | solution.py:25
  64.7 14.3 %collective-permute-start.35 = (bf16[1024,128]{1,0:T(8,128)(2,1)}, bf16[1024,128]{1,0:T(8,128)(2,1)S(1)}, u32[]{:S(2)}, u32[]{:S(2)}) collective-permute-start(bf16[1024,128]{1,0:T(8,128)(2,1)} %refs_8_.1), channel_id=1, source_target_pairs={{0,4},{1,5},{2,6},{3,7},{4,0},{5,1},{6,2},{7,3},{8,12},{9,13},{10,... | collective-permute-start | bytes 786440 | tf_op jit(solution)/shard_map/ppermute | solution.py:25
  65.0 0.7 copy-start.28
  67.3 14.2 %collective-permute-start.37 = (bf16[1024,128]{1,0:T(8,128)(2,1)}, bf16[1024,128]{1,0:T(8,128)(2,1)}, u32[]{:S(2)}, u32[]{:S(2)}) collective-permute-start(bf16[1024,128]{1,0:T(8,128)(2,1)} %refs_8_.1), channel_id=1, source_target_pairs={{0,6},{1,7},{2,4},{3,5},{4,2},{5,3},{6,0},{7,1},{8,14},{9,15},{10,... | collective-permute-start | bytes 786440 | tf_op jit(solution)/shard_map/ppermute | solution.py:25
  69.5 12.6 %collective-permute-start.21 = (bf16[8,128,128]{2,1,0:T(8,128)(2,1)}, bf16[8,128,128]{2,1,0:T(8,128)(2,1)}, u32[]{:S(2)}, u32[]{:S(2)}) collective-permute-start(bf16[8,128,128]{2,1,0:T(8,128)(2,1)} %get-tuple-element.49), channel_id=1, source_target_pairs={{24,0},{0,8},{8,16},{16,24},{25,1},{1,9},{9,17},{17,25},{26,2},{2,... | collective-permute-start | bytes 786440 | tf_op jit(solution)/shard_map/ppermute | solution.py:20
  71.1 13.6 %collective-permute-start.22 = (bf16[8,128,128]{2,1,0:T(8,128)(2,1)}, bf16[8,128,128]{2,1,0:T(8,128)(2,1)}, u32[]{:S(2)}, u32[]{:S(2)}) collective-permute-start(bf16[8,128,128]{2,1,0:T(8,128)(2,1)} %get-tuple-element.50), channel_id=1, source_target_pairs={{8,0},{16,8},{24,16},{0,24},{9,1},{17,9},{25,17},{1,25},{10,2},{18... | collective-permute-start | bytes 786440 | tf_op jit(solution)/shard_map/ppermute | solution.py:20
  73.4 5.7 %copy-start.6 = (bf16[1024,128]{1,0:T(8,128)(2,1)}, bf16[1024,128]{1,0:T(8,128)(2,1)S(1)}, u32[]{:S(2)}) copy-start(bf16[1024,128]{1,0:T(8,128)(2,1)S(1)} %collective-permute-done.33.refs_10_) | copy-start | bytes 786436
  73.4 13.8 %collective-permute-start.2 = (bf16[128,1024]{1,0:T(8,128)(2,1)S(1)}, bf16[128,1024]{1,0:T(8,128)(2,1)}, u32[]{:S(2)}, u32[]{:S(2)}) collective-permute-start(bf16[128,1024]{1,0:T(8,128)(2,1)S(1)} %collective-permute-done.1.refs_2_), channel_id=1, source_target_pairs={{0,1},{1,0},{2,3},{3,2},{4,5},{5,4},{6,7},{7,6},{8,9},{9,8},{10,11... | collective-permute-start | bytes 786440 | tf_op jit(solution)/shard_map/ppermute | solution.py:25
  79.1 0.7 copy-start.8
  79.8 7.4 %collective-permute-start.4 = (bf16[128,1024]{1,0:T(8,128)(2,1)S(1)}, bf16[128,1024]{1,0:T(8,128)(2,1)}, u32[]{:S(2)}, u32[]{:S(2)}) collective-permute-start(bf16[128,1024]{1,0:T(8,128)(2,1)S(1)} %collective-permute-done.3.refs_4_), channel_id=1, source_target_pairs={{0,1},{1,0},{2,3},{3,2},{4,5},{5,4},{6,7},{7,6},{8,9},{9,8},{10,11... | collective-permute-start | bytes 786440 | tf_op jit(solution)/shard_map/ppermute | solution.py:25
  79.8 7.4 %copy-start.7 = (bf16[1024,128]{1,0:T(8,128)(2,1)S(1)}, bf16[1024,128]{1,0:T(8,128)(2,1)}, u32[]{:S(2)}) copy-start(bf16[1024,128]{1,0:T(8,128)(2,1)} %copy-done.6) | copy-start | bytes 786436
  79.8 7.9 %copy-start.9 = (bf16[1024,128]{1,0:T(8,128)(2,1)S(1)}, bf16[1024,128]{1,0:T(8,128)(2,1)}, u32[]{:S(2)}) copy-start(bf16[1024,128]{1,0:T(8,128)(2,1)} %copy-done.8) | copy-start | bytes 786436
  81.5 6.1 %collective-permute-start.6 = (bf16[128,1024]{1,0:T(8,128)(2,1)S(1)}, bf16[128,1024]{1,0:T(8,128)(2,1)S(1)}, u32[]{:S(2)}, u32[]{:S(2)}) collective-permute-start(bf16[128,1024]{1,0:T(8,128)(2,1)S(1)} %collective-permute-done.5.refs_6_), channel_id=1, source_target_pairs={{0,1},{1,0},{2,3},{3,2},{4,5},{5,4},{6,7},{7,6},{8,9},{9,8},{10,11... | collective-permute-start | bytes 786440 | tf_op jit(solution)/shard_map/ppermute | solution.py:25
  82.1 12.1 %collective-permute-start.23 = (bf16[8,128,128]{2,1,0:T(8,128)(2,1)S(1)}, bf16[8,128,128]{2,1,0:T(8,128)(2,1)S(1)}, u32[]{:S(2)}, u32[]{:S(2)}) collective-permute-start(bf16[8,128,128]{2,1,0:T(8,128)(2,1)S(1)} %get-tuple-element.51), channel_id=1, source_target_pairs={{24,0},{0,8},{8,16},{16,24},{25,1},{1,9},{9,17},{17,25},{26,2},{2,... | collective-permute-start | bytes 786440 | tf_op jit(solution)/shard_map/ppermute | solution.py:20
  84.7 10.9 %copy-start.11 = (bf16[128,384]{1,0:T(8,128)(2,1)S(1)}, bf16[128,384]{1,0:T(8,128)(2,1)}, u32[]{:S(2)}) copy-start(bf16[128,384]{1,0:T(8,128)(2,1)} %copy-done.10) | copy-start | bytes 294916
  84.7 10.9 %copy-start.13 = (bf16[128,384]{1,0:T(8,128)(2,1)S(1)}, bf16[128,384]{1,0:T(8,128)(2,1)}, u32[]{:S(2)}) copy-start(bf16[128,384]{1,0:T(8,128)(2,1)} %copy-done.12) | copy-start | bytes 294916
  84.7 10.9 %copy-start.15 = (bf16[128,384]{1,0:T(8,128)(2,1)S(1)}, bf16[128,384]{1,0:T(8,128)(2,1)}, u32[]{:S(2)}) copy-start(bf16[128,384]{1,0:T(8,128)(2,1)} %copy-done.14) | copy-start | bytes 294916
  84.7 11.0 %copy-start.17 = (bf16[128,384]{1,0:T(8,128)(2,1)S(1)}, bf16[128,384]{1,0:T(8,128)(2,1)}, u32[]{:S(2)}) copy-start(bf16[128,384]{1,0:T(8,128)(2,1)} %copy-done.16) | copy-start | bytes 294916
  84.7 11.0 %copy-start.19 = (bf16[128,384]{1,0:T(8,128)(2,1)S(1)}, bf16[128,384]{1,0:T(8,128)(2,1)}, u32[]{:S(2)}) copy-start(bf16[128,384]{1,0:T(8,128)(2,1)} %copy-done.18) | copy-start | bytes 294916
  84.7 11.0 %copy-start.21 = (bf16[128,384]{1,0:T(8,128)(2,1)S(1)}, bf16[128,384]{1,0:T(8,128)(2,1)}, u32[]{:S(2)}) copy-start(bf16[128,384]{1,0:T(8,128)(2,1)} %copy-done.20) | copy-start | bytes 294916
  84.7 11.0 %copy-start.23 = (bf16[128,384]{1,0:T(8,128)(2,1)S(1)}, bf16[128,384]{1,0:T(8,128)(2,1)}, u32[]{:S(2)}) copy-start(bf16[128,384]{1,0:T(8,128)(2,1)} %copy-done.22) | copy-start | bytes 294916
  84.7 11.0 %copy-start.25 = (bf16[128,384]{1,0:T(8,128)(2,1)S(1)}, bf16[128,384]{1,0:T(8,128)(2,1)}, u32[]{:S(2)}) copy-start(bf16[128,384]{1,0:T(8,128)(2,1)} %copy-done.24) | copy-start | bytes 294916
  84.8 14.6 %collective-permute-start.24 = (bf16[8,128,128]{2,1,0:T(8,128)(2,1)S(1)}, bf16[8,128,128]{2,1,0:T(8,128)(2,1)S(1)}, u32[]{:S(2)}, u32[]{:S(2)}) collective-permute-start(bf16[8,128,128]{2,1,0:T(8,128)(2,1)S(1)} %get-tuple-element.52), channel_id=1, source_target_pairs={{8,0},{16,8},{24,16},{0,24},{9,1},{17,9},{25,17},{1,25},{10,2},{18... | collective-permute-start | bytes 786440 | tf_op jit(solution)/shard_map/ppermute | solution.py:20
  87.1 17.7 %collective-permute-start.32 = (bf16[1024,128]{1,0:T(8,128)(2,1)}, bf16[1024,128]{1,0:T(8,128)(2,1)S(1)}, u32[]{:S(2)}, u32[]{:S(2)}) collective-permute-start(bf16[1024,128]{1,0:T(8,128)(2,1)} %refs_8_.1), channel_id=1, source_target_pairs={{0,1},{1,0},{2,3},{3,2},{4,5},{5,4},{6,7},{7,6},{8,9},{9,8},{10,11... | collective-permute-start | bytes 786440 | tf_op jit(solution)/shard_map/ppermute | solution.py:25
  87.2 18.8 %collective-permute-start.34 = (bf16[1024,128]{1,0:T(8,128)(2,1)S(1)}, bf16[1024,128]{1,0:T(8,128)(2,1)S(1)}, u32[]{:S(2)}, u32[]{:S(2)}) collective-permute-start(bf16[1024,128]{1,0:T(8,128)(2,1)S(1)} %copy-done.7), channel_id=1, source_target_pairs={{0,1},{1,0},{2,3},{3,2},{4,5},{5,4},{6,7},{7,6},{8,9},{9,8},{10,11... | collective-permute-start | bytes 786440 | tf_op jit(solution)/shard_map/ppermute | solution.py:25
  87.7 18.6 %collective-permute-start.36 = (bf16[1024,128]{1,0:T(8,128)(2,1)S(1)}, bf16[1024,128]{1,0:T(8,128)(2,1)S(1)}, u32[]{:S(2)}, u32[]{:S(2)}) collective-permute-start(bf16[1024,128]{1,0:T(8,128)(2,1)S(1)} %copy-done.9), channel_id=1, source_target_pairs={{0,1},{1,0},{2,3},{3,2},{4,5},{5,4},{6,7},{7,6},{8,9},{9,8},{10,11... | collective-permute-start | bytes 786440 | tf_op jit(solution)/shard_map/ppermute | solution.py:25
  94.2 12.4 %collective-permute-start.38 = (bf16[1024,128]{1,0:T(8,128)(2,1)}, bf16[1024,128]{1,0:T(8,128)(2,1)S(1)}, u32[]{:S(2)}, u32[]{:S(2)}) collective-permute-start(bf16[1024,128]{1,0:T(8,128)(2,1)} %collective-permute-done.37.refs_14_), channel_id=1, source_target_pairs={{0,1},{1,0},{2,3},{3,2},{4,5},{5,4},{6,7},{7,6},{8,9},{9,8},{10,11... | collective-permute-start | bytes 786440 | tf_op jit(solution)/shard_map/ppermute | solution.py:25
  99.3 0.7 copy-start.29
  104.3 4.1 %collective-permute-start.25 = (bf16[128,128]{1,0:T(8,128)(2,1)S(1)}, bf16[128,128]{1,0:T(8,128)(2,1)S(1)}, u32[]{:S(2)}, u32[]{:S(2)}) collective-permute-start(bf16[128,128]{1,0:T(8,128)(2,1)S(1)} %get-tuple-element.54), channel_id=1, source_target_pairs={{0,1},{1,0},{2,3},{3,2},{4,5},{5,4},{6,7},{7,6},{8,9},{9,8},{10,11... | collective-permute-start | bytes 98312 | tf_op jit(solution)/shard_map/ppermute | solution.py:25
  104.8 4.4 %collective-permute-start.26 = (bf16[128,128]{1,0:T(8,128)(2,1)S(1)}, bf16[128,128]{1,0:T(8,128)(2,1)S(1)}, u32[]{:S(2)}, u32[]{:S(2)}) collective-permute-start(bf16[128,128]{1,0:T(8,128)(2,1)S(1)} %get-tuple-element.55), channel_id=1, source_target_pairs={{0,2},{1,3},{2,0},{3,1},{4,6},{5,7},{6,4},{7,5},{8,10},{9,11},{10,... | collective-permute-start | bytes 98312 | tf_op jit(solution)/shard_map/ppermute | solution.py:25
  105.9 4.8 %collective-permute-start.27 = (bf16[128,128]{1,0:T(8,128)(2,1)S(1)}, bf16[128,128]{1,0:T(8,128)(2,1)S(1)}, u32[]{:S(2)}, u32[]{:S(2)}) collective-permute-start(bf16[128,128]{1,0:T(8,128)(2,1)S(1)} %get-tuple-element.56), channel_id=1, source_target_pairs={{0,3},{1,2},{2,1},{3,0},{4,7},{5,6},{6,5},{7,4},{8,11},{9,10},{10,... | collective-permute-start | bytes 98312 | tf_op jit(solution)/shard_map/ppermute | solution.py:25
  106.3 4.4 %collective-permute-start.28 = (bf16[128,128]{1,0:T(8,128)(2,1)S(1)}, bf16[128,128]{1,0:T(8,128)(2,1)S(1)}, u32[]{:S(2)}, u32[]{:S(2)}) collective-permute-start(bf16[128,128]{1,0:T(8,128)(2,1)S(1)} %get-tuple-element.57), channel_id=1, source_target_pairs={{0,4},{1,5},{2,6},{3,7},{4,0},{5,1},{6,2},{7,3},{8,12},{9,13},{10,... | collective-permute-start | bytes 98312 | tf_op jit(solution)/shard_map/ppermute | solution.py:25
  106.6 4.1 %collective-permute-start.29 = (bf16[128,128]{1,0:T(8,128)(2,1)S(1)}, bf16[128,128]{1,0:T(8,128)(2,1)S(1)}, u32[]{:S(2)}, u32[]{:S(2)}) collective-permute-start(bf16[128,128]{1,0:T(8,128)(2,1)S(1)} %get-tuple-element.58), channel_id=1, source_target_pairs={{0,5},{1,4},{2,7},{3,6},{4,1},{5,0},{6,3},{7,2},{8,13},{9,12},{10,... | collective-permute-start | bytes 98312 | tf_op jit(solution)/shard_map/ppermute | solution.py:25
  108.3 4.9 %collective-permute-start.30 = (bf16[128,128]{1,0:T(8,128)(2,1)S(1)}, bf16[128,128]{1,0:T(8,128)(2,1)S(1)}, u32[]{:S(2)}, u32[]{:S(2)}) collective-permute-start(bf16[128,128]{1,0:T(8,128)(2,1)S(1)} %get-tuple-element.59), channel_id=1, source_target_pairs={{0,6},{1,7},{2,4},{3,5},{4,2},{5,3},{6,0},{7,1},{8,14},{9,15},{10,... | collective-permute-start | bytes 98312 | tf_op jit(solution)/shard_map/ppermute | solution.py:25
  109.2 4.6 %collective-permute-start.31 = (bf16[128,128]{1,0:T(8,128)(2,1)S(1)}, bf16[128,128]{1,0:T(8,128)(2,1)S(1)}, u32[]{:S(2)}, u32[]{:S(2)}) collective-permute-start(bf16[128,128]{1,0:T(8,128)(2,1)S(1)} %get-tuple-element.60), channel_id=1, source_target_pairs={{0,7},{1,6},{2,5},{3,4},{4,3},{5,2},{6,1},{7,0},{8,15},{9,14},{10,... | collective-permute-start | bytes 98312 | tf_op jit(solution)/shard_map/ppermute | solution.py:25
  (6 other events, 3.8 us)

commit v2 on v1

--- a/solution.py
+++ b/solution.py
@@ -1,3 +1,5 @@
+import math
+
 import jax
 import jax.numpy as jnp
 from jax import lax
@@ -35,10 +37,6 @@
 
 def exchanged(pieces):
     return [pieces[0]] + [partner(pieces[m], m) for m in range(1, len(pieces))]
-
-
-def swapped(pieces):
-    return lax.all_to_all(pieces, "tok", split_axis=0, concat_axis=0, tiled=True)
 
 
 def kernel(body, arguments, out_shape, in_specs, out_specs, scratch, limit, flops, moved):
@@ -99,7 +97,13 @@
     )
 
 
-def pick_sides(pieces, tables, n_region, n_tok):
+def cached_at(list_ref, entry, query_block, n_tok):
+    max_entries = list_ref.shape[0] // 2 - 1
+    slot = list_ref[2 * max_entries + 1, list_ref[entry, query_block]]
+    return lax.rem(slot, n_tok), list_ref[max_entries + entry, query_block]
+
+
+def pick_sides(pieces, lists, n_region, n_tok):
     whole = not isinstance(pieces, list)
     _, rows, head_size = pieces.shape[1:] if whole else pieces[0].shape
     dtype = pieces.dtype if whole else pieces[0].dtype
@@ -110,7 +114,7 @@
         lower = lax.rem(region_id + n_region - 1, n_region)
         return (0, upper), (1, lower)
 
-    def body(block_ref, frame_ref, slot_ref, *refs):
+    def body(list_ref, *refs):
         piece_refs = refs[: -4 if not whole else 1]
         up_ref, down_ref, places, sems = refs[-4:]
         tok_id = lax.axis_index("tok")
@@ -118,9 +122,7 @@
         for (entry, reader), out_ref in zip(neighbours(), (up_ref, down_ref)):
             for m in range(n_tok):
                 query_block = reader * n_tok + (tok_id ^ m)
-                slot = slot_ref[block_ref[entry, query_block]]
-                source = lax.rem(slot, n_tok)
-                frame = frame_ref[entry, query_block]
+                source, frame = cached_at(list_ref, entry, query_block, n_tok)
                 if whole:
                     copies.append(
                         pltpu.make_async_copy(
@@ -147,9 +149,9 @@
     side = jax.ShapeDtypeStruct((n_tok, rows, head_size), dtype)
     return kernel(
         body,
-        tables + ((pieces,) if whole else tuple(pieces)),
+        (lists, pieces) if whole else (lists, *pieces),
         [side, side],
-        [SMEM] * 3 + [ANY] * (1 if whole else n_tok),
+        [SMEM] + [ANY] * (1 if whole else n_tok),
         [ANY] * 2,
         [pltpu.SMEM((2, n_tok), jnp.int32), pltpu.SemaphoreType.DMA((2, n_tok))],
         4,
@@ -163,98 +165,92 @@
     rows, width = token_blocks[0].shape
     depth, columns = weight_rows[0].shape
     dtype = token_blocks[0].dtype
-    n_chunks = 2
-    chunk = n_tok // n_chunks
 
     def body(*refs):
         token_refs = refs[:n_tok]
         weight_refs = refs[n_tok : 2 * n_tok]
-        out_ref, held, whole, sems = refs[2 * n_tok :]
+        out_ref, whole = refs[2 * n_tok :]
         tok_id = lax.axis_index("tok")
-        weight_copies = []
         for m in range(n_tok):
             start = pl.multiple_of((tok_id ^ m) * depth, depth)
-            target = whole.at[pl.ds(start, depth), :]
-            weight_copies.append(pltpu.make_async_copy(weight_refs[m], target, sems.at[0, m]))
-            weight_copies[-1].start()
-        token_copies = []
-        for m in range(n_tok):
-            target = held.at[m * rows : (m + 1) * rows]
-            token_copies.append(pltpu.make_async_copy(token_refs[m], target, sems.at[1, m]))
-            token_copies[-1].start()
-        for copy in weight_copies:
-            copy.wait()
-        for c in range(n_chunks):
-            for m in range(c * chunk, (c + 1) * chunk):
-                token_copies[m].wait()
-            some = slice(c * chunk * rows, (c + 1) * chunk * rows)
-            out_ref[some] = jnp.dot(
-                held[some], whole[...], preferred_element_type=jnp.float32
-            ).astype(dtype)
+            whole[pl.ds(start, depth), :] = weight_refs[m][...]
+        tokens = jnp.concatenate([ref[...] for ref in token_refs], 0)
+        out_ref[...] = jnp.dot(
+            tokens, whole[...], preferred_element_type=jnp.float32
+        ).astype(dtype)
 
     out = kernel(
         body,
         (*token_blocks, *weight_rows),
         jax.ShapeDtypeStruct((n_tok * rows, columns), dtype),
-        [ANY] * (2 * n_tok),
+        [VMEM] * (2 * n_tok),
         VMEM,
-        [
-            pltpu.VMEM((n_tok * rows, width), dtype),
-            pltpu.VMEM((n_tok * depth, columns), dtype),
-            pltpu.SemaphoreType.DMA((2, n_tok)),
-        ],
-        12,
+        [pltpu.VMEM((n_tok * depth, columns), dtype)],
+        14,
         2 * n_tok * rows * width * columns,
         2 * n_tok * (rows * width + depth * columns),
     )
     return out.reshape(n_tok, rows, columns)
 
 
-def attend(projected, keys, values, side_keys, side_values, tables, counts):
+def attend(projected, keys, values, side_keys, side_values, lists):
     n_tok, rows, columns = projected.shape
     head_size = columns // 3
-    frames = keys.shape[1]
-    max_entries = tables[0].shape[0]
-    scale = head_size ** (-0.5)
+    frames = values.shape[1]
+    max_entries = lists.shape[0] // 2 - 1
+    length = (max_entries + 1) * rows
+    base = head_size ** (-0.5) * math.log2(math.e)
     across = (((1,), (1,)), ((), ()))
-
-    def body(block_ref, frame_ref, slot_ref, count_ref, proj_ref, key_ref, value_ref, *refs):
+    chunk = 32
+    always = 3
+
+    def body(list_ref, proj_ref, key_ref, value_ref, *refs):
         side_refs = refs[:4]
-        out_refs = refs[4:]
+        out_refs = refs[4 : 4 + n_tok]
+        score_ref, prob_ref = refs[4 + n_tok :]
         region_id = lax.axis_index("region")
         tok_id = lax.axis_index("tok")
+
+        def listed(m, own, sides, cached_ref):
+            query_block = region_id * n_tok + (tok_id ^ m)
+            found = [own] + [side[m] for side in sides]
+            for entry in range(2, max_entries):
+                source, frame = cached_at(list_ref, entry, query_block, n_tok)
+                found.append(cached_ref[source ^ tok_id, frame])
+            return jnp.concatenate(found, 0)
+
+        def score(m):
+            score_ref[m % 2] = lax.dot_general(
+                proj_ref[m, :, :head_size],
+                listed(m, proj_ref[m, :, head_size : 2 * head_size], side_refs[:2], key_ref),
+                across,
+                preferred_element_type=jnp.float32,
+            )
+
+        def soften(m):
+            live = list_ref[2 * max_entries, region_id * n_tok + (tok_id ^ m)]
+            totals = []
+            for row in range(0, rows, chunk):
+                some = slice(row, row + chunk)
+                blocks = [score_ref[m % 2, some, : always * rows]]
+                for entry in range(always - 1, max_entries):
+                    block = score_ref[m % 2, some, (entry + 1) * rows : (entry + 2) * rows]
+                    blocks.append(jnp.where(entry < live, block, jnp.float32(-1e30)))
+                scores = jnp.concatenate(blocks, 1)
+                row_max = jnp.max(scores, axis=1, keepdims=True)
+                weights = jnp.exp2((scores - row_max) * base)
+                totals.append(jnp.sum(weights, axis=1, keepdims=True))
+                prob_ref[m % 2, some] = weights.astype(jnp.bfloat16)
+            return jnp.concatenate(totals, 0)
+
+        score(0)
         for m in range(n_tok):
-            query_block = region_id * n_tok + (tok_id ^ m)
-            live = count_ref[query_block]
-            query = proj_ref[m, :, :head_size]
-            key_list = [proj_ref[m, :, head_size : 2 * head_size]]
-            value_list = [proj_ref[m, :, 2 * head_size :]]
-            for entry in range(2):
-                key_list.append(side_refs[entry][m])
-                value_list.append(side_refs[2 + entry][m])
-            for entry in range(2, max_entries):
-                slot = slot_ref[block_ref[entry, query_block]]
-                source = lax.rem(slot, n_tok)
-                frame = frame_ref[entry, query_block]
-                key_list.append(key_ref[source ^ tok_id, frame])
-                value_list.append(value_ref[source, frame])
-            scores = (
-                lax.dot_general(
-                    query,
-                    jnp.concatenate(key_list, 0),
-                    across,
-                    preferred_element_type=jnp.float32,
-                )
-                * scale
-            )
-            column = lax.broadcasted_iota(jnp.int32, scores.shape, 1)
-            scores = jnp.where(column < (live + 1) * rows, scores, jnp.float32(-1e30))
-            row_max = jnp.max(scores, axis=1, keepdims=True)
-            weights = jnp.exp(scores - row_max)
-            total = jnp.sum(weights, axis=1, keepdims=True)
+            if m + 1 < n_tok:
+                score(m + 1)
+            total = soften(m)
             context = jnp.dot(
-                weights.astype(jnp.bfloat16),
-                jnp.concatenate(value_list, 0),
+                prob_ref[m % 2],
+                listed(m, proj_ref[m, :, 2 * head_size :], side_refs[2:], value_ref),
                 preferred_element_type=jnp.float32,
             )
             out_refs[m][...] = (context / total).astype(out_refs[m].dtype)
@@ -262,13 +258,16 @@
     dtype = projected.dtype
     return kernel(
         body,
-        (*tables, counts, projected, keys, values, *side_keys, *side_values),
+        (lists, projected, keys, values, *side_keys, *side_values),
         [jax.ShapeDtypeStruct((rows, head_size), dtype)] * n_tok,
-        [SMEM] * 4 + [VMEM] * 7,
+        [SMEM] + [VMEM] * 7,
         [VMEM] * n_tok,
-        [],
+        [
+            pltpu.VMEM((2, rows, length), jnp.float32),
+            pltpu.VMEM((2, rows, length), dtype),
+        ],
         16,
-        4 * n_tok * rows * rows * (max_entries + 1) * head_size,
+        4 * n_tok * rows * length * head_size,
         4 * n_tok * frames * rows * head_size,
     )
 
@@ -292,7 +291,7 @@
         tuple(pieces),
         jax.ShapeDtypeStruct((n_pieces,) + piece.shape, piece.dtype),
         [ANY] * n_pieces,
-        ANY,
+        VMEM,
         [pltpu.SemaphoreType.DMA((n_pieces,))],
         4,
         0,
@@ -309,25 +308,14 @@
     def body(*refs):
         context_refs = refs[:n_tok]
         column_refs = refs[n_tok : 2 * n_tok]
-        out_ref, context, held, sems = refs[2 * n_tok :]
-        copies = [
-            pltpu.make_async_copy(
-                column_refs[m],
-                held.at[m // 2, :, m % 2 * columns : (m % 2 + 1) * columns],
-                sems.at[m],
-            )
-            for m in range(n_tok)
-        ]
-        for copy in copies:
-            copy.start()
+        out_ref, context = refs[2 * n_tok :]
         tok_id = lax.axis_index("tok")
         for m in range(n_tok):
             start = pl.multiple_of((tok_id ^ m) * head_size, head_size)
             context[:, pl.ds(start, head_size)] = context_refs[m][...]
         for m in range(0, n_tok, 2):
-            copies[m].wait()
-            copies[m + 1].wait()
-            mixed = jnp.dot(context[...], held[m // 2], preferred_element_type=jnp.float32)
+            pair = jnp.concatenate([column_refs[m][...], column_refs[m + 1][...]], 1)
+            mixed = jnp.dot(context[...], pair, preferred_element_type=jnp.float32)
             for j in range(2):
                 start = pl.multiple_of((tok_id ^ (m + j)) * columns, columns)
                 out_ref[:, pl.ds(start, columns)] = mixed[
@@ -338,13 +326,9 @@
         body,
         (*context_heads, *out_columns),
         jax.ShapeDtypeStruct((rows, n_tok * columns), dtype),
-        [VMEM] * n_tok + [ANY] * n_tok,
+        [VMEM] * (2 * n_tok),
         VMEM,
-        [
-            pltpu.VMEM((rows, n_tok * head_size), dtype),
-            pltpu.VMEM((n_tok // 2, width, 2 * columns), dtype),
-            pltpu.SemaphoreType.DMA((n_tok,)),
-        ],
+        [pltpu.VMEM((rows, n_tok * head_size), dtype)],
         12,
         2 * rows * width * n_tok * columns,
         2 * width * n_tok * columns,
@@ -366,13 +350,15 @@
 ):
     n_region = lax.axis_size("region")
     n_tok = lax.axis_size("tok")
-    tables = (nb_block.T, nb_frame.T, block_slot)
+    lists = jnp.concatenate(
+        [nb_block.T, nb_frame.T, nb_count[None], block_slot[None]], 0
+    )
     keys = exchanged(pack((past_keys,), n_tok, True))
-    values = swapped(pack((past_values,), n_tok, False))
-    up_keys, down_keys = pick_sides(keys, tables, n_region, n_tok)
+    values = exchanged(pack((past_values,), n_tok, True))
+    up_keys, down_keys = pick_sides(keys, lists, n_region, n_tok)
     below_keys = shifted(up_keys, "region", 1)
     above_keys = shifted(down_keys, "region", -1)
-    up_values, down_values = pick_sides(values, tables, n_region, n_tok)
+    up_values, down_values = pick_sides(values, lists, n_region, n_tok)
     below_values = shifted(up_values, "region", 1)
     above_values = shifted(down_values, "region", -1)
     weight_rows = exchanged(pack((w_query, w_key, w_value), n_tok, True))
@@ -382,11 +368,10 @@
     context = attend(
         projected,
         join(keys),
-        values,
+        join(values),
         (below_keys, above_keys),
         (below_values, above_values),
-        tables,
-        nb_count,
+        lists,
     )
     return mix(exchanged(context), out_columns)
 

time: 118 us -> 102 us (0.86); the launches traced: 117 us -> 102 us
  waiting for transfers between devices: 50.9 us -> 39.3 us
  Pallas kernels: 17.5 us -> 13.3 us
  starting transfers between devices: 40.2 us -> 44.4 us
  local copies, waits for them, and re-layouts: 7.72 us -> 4.75 us
    ppermute x35 -> x42, starting transfers between devices: 27.1 us -> 38.3 us  [partner(): return lax.ppermute(block, 'tok', route)]
    ppermute x35 -> x42, waiting for transfers between devices: 43.4 us -> 32.3 us  [partner(): return lax.ppermute(block, 'tok', route)]
    all_to_all x1 -> x0, starting transfers between devices: 5.34 us -> none  [swapped(): lax.all_to_all(pieces, 'tok', split_axis=0, concat_axis=0, tiled=True)]
    pallas_call x9 -> x10, Pallas kernels: 17.5 us -> 13.3 us  [kernel(): pl.pallas_call(body, out_shape=out_shape, in_specs=in_specs, out_specs=ou...]
    unnamed x60 -> x22, local copies, waits for them, and re-layouts: 7.72 us -> 4.75 us
    ppermute x4, starting transfers between devices: 7.78 us -> 6.16 us  [shifted(): return lax.ppermute(block, axis, route)]
  transfers between devices with their start and end apart: 40 -> 46, of which waited for: 9 -> 15; matrix products, arithmetic and copies ran while one was open for 0% -> 0% of each run, Pallas kernels for 12% -> 11%
where the time goes in v2:
time: 102 us
  starting transfers between devices  44.4 us (44%)
  waiting for transfers between devices  39.3 us (39%)
  Pallas kernels  13.3 us (13%)
  local copies, waits for them, and re-layouts  4.75 us (5%)
    ppermute x42, starting transfers between devices, partner(): return lax.ppermute(block, 'tok', route)  38.3 us
    ppermute x42, waiting for transfers between devices, partner(): return lax.ppermute(block, 'tok', route)  32.3 us
    pallas_call x10, Pallas kernels, kernel(): pl.pallas_call(body, out_shape=out_shape, in_specs=in_specs, out_specs=ou...  13.3 us
    ppermute x4, waiting for transfers between devices, shifted(): return lax.ppermute(block, axis, route)  6.98 us
    ppermute x4, starting transfers between devices, shifted(): return lax.ppermute(block, axis, route)  6.16 us
    unnamed x22, local copies, waits for them, and re-layouts  4.75 us
  transfers between devices with their start and end apart: 46, of which 15 were waited for; matrix products, arithmetic and copies ran while one was open for 0% of the time, Pallas kernels for 11%

profile of v2, /device:TPU:0, one launch (start us, length us, event | category | flops | bytes accessed | tf_op | source)
XLA Modules:
  0.0 102.0 jit_solution(4441008272066079132)
XLA Ops:
  0.0 0.9 copy-done.3
  1.0 0.9 copy-done.4
  1.9 0.9 copy-done.5
  2.9 0.5 shard_map.109
  3.4 0.6 collective-permute-start.7
  3.9 2.6 %collective-permute-start.8 = (bf16[128,384]{1,0:T(8,128)(2,1)S(1)}, bf16[128,384]{1,0:T(8,128)(2,1)S(1)}, u32[]{:S(2)}, u32[]{:S(2)}) collective-permute-start(bf16[128,384]{1,0:T(8,128)(2,1)S(1)} %get-tuple-element.43), channel_id=1, source_target_pairs={{0,2},{1,3},{2,0},{3,1},{4,6},{5,7},{6,4},{7,5},{8,10},{9,11},{10,... | collective-permute-start | bytes 294920 | tf_op jit(solution)/shard_map/ppermute | solution.py:27
  6.5 1.8 %collective-permute-start.10 = (bf16[128,384]{1,0:T(8,128)(2,1)S(1)}, bf16[128,384]{1,0:T(8,128)(2,1)S(1)}, u32[]{:S(2)}, u32[]{:S(2)}) collective-permute-start(bf16[128,384]{1,0:T(8,128)(2,1)S(1)} %get-tuple-element.45), channel_id=1, source_target_pairs={{0,4},{1,5},{2,6},{3,7},{4,0},{5,1},{6,2},{7,3},{8,12},{9,13},{10,... | collective-permute-start | bytes 294920 | tf_op jit(solution)/shard_map/ppermute | solution.py:27
  8.3 1.2 %copy-done = bf16[4,128,1024]{2,1,0:T(8,128)(2,1)S(1)} copy-done((bf16[4,128,1024]{2,1,0:T(8,128)(2,1)S(1)}, bf16[4,128,1024]{2,1,0:T(8,128)(2,1)}, u32[]{:S(2)}) %copy-start) | copy-done | bytes 1048600
  9.5 0.4 shard_map.111
  9.9 0.1 collective-permute-start.14
  10.0 1.5 %collective-permute-start.15 = (bf16[4,128,128]{2,1,0:T(8,128)(2,1)S(1)}, bf16[4,128,128]{2,1,0:T(8,128)(2,1)S(1)}, u32[]{:S(2)}, u32[]{:S(2)}) collective-permute-start(bf16[4,128,128]{2,1,0:T(8,128)(2,1)S(1)} %get-tuple-element.51), channel_id=1, source_target_pairs={{0,2},{1,3},{2,0},{3,1},{4,6},{5,7},{6,4},{7,5},{8,10},{9,11},{10,... | collective-permute-start | bytes 393224 | tf_op jit(solution)/shard_map/ppermute | solution.py:27
  11.5 0.3 collective-permute-start.11
  11.8 2.3 %collective-permute-start.12 = (bf16[128,384]{1,0:T(8,128)(2,1)S(1)}, bf16[128,384]{1,0:T(8,128)(2,1)S(1)}, u32[]{:S(2)}, u32[]{:S(2)}) collective-permute-start(bf16[128,384]{1,0:T(8,128)(2,1)S(1)} %get-tuple-element.47), channel_id=1, source_target_pairs={{0,6},{1,7},{2,4},{3,5},{4,2},{5,3},{6,0},{7,1},{8,14},{9,15},{10,... | collective-permute-start | bytes 294920 | tf_op jit(solution)/shard_map/ppermute | solution.py:27
  14.1 0.4 collective-permute-start.13
  14.5 6.0 %collective-permute-done.11.refs_13_ = bf16[128,384]{1,0:T(8,128)(2,1)S(1)} collective-permute-done((bf16[128,384]{1,0:T(8,128)(2,1)S(1)}, bf16[128,384]{1,0:T(8,128)(2,1)S(1)}, u32[]{:S(2)}, u32[]{:S(2)}) %collective-permute-start.11) | collective-permute-done | bytes 98336 | tf_op jit(solution)/shard_map/ppermute | solution.py:27
  20.5 1.5 %collective-permute-start.18 = (bf16[4,128,128]{2,1,0:T(8,128)(2,1)S(1)}, bf16[4,128,128]{2,1,0:T(8,128)(2,1)S(1)}, u32[]{:S(2)}, u32[]{:S(2)}) collective-permute-start(bf16[4,128,128]{2,1,0:T(8,128)(2,1)S(1)} %get-tuple-element.54), channel_id=1, source_target_pairs={{0,5},{1,4},{2,7},{3,6},{4,1},{5,0},{6,3},{7,2},{8,13},{9,12},{10,... | collective-permute-start | bytes 393224 | tf_op jit(solution)/shard_map/ppermute | solution.py:27
  22.0 1.8 %collective-permute-start.19 = (bf16[4,128,128]{2,1,0:T(8,128)(2,1)S(1)}, bf16[4,128,128]{2,1,0:T(8,128)(2,1)S(1)}, u32[]{:S(2)}, u32[]{:S(2)}) collective-permute-start(bf16[4,128,128]{2,1,0:T(8,128)(2,1)S(1)} %get-tuple-element.55), channel_id=1, source_target_pairs={{0,6},{1,7},{2,4},{3,5},{4,2},{5,3},{6,0},{7,1},{8,14},{9,15},{10,... | collective-permute-start | bytes 393224 | tf_op jit(solution)/shard_map/ppermute | solution.py:27
  23.8 1.1 %collective-permute-start.20 = (bf16[4,128,128]{2,1,0:T(8,128)(2,1)S(1)}, bf16[4,128,128]{2,1,0:T(8,128)(2,1)S(1)}, u32[]{:S(2)}, u32[]{:S(2)}) collective-permute-start(bf16[4,128,128]{2,1,0:T(8,128)(2,1)S(1)} %get-tuple-element.56), channel_id=1, source_target_pairs={{0,7},{1,6},{2,5},{3,4},{4,3},{5,2},{6,1},{7,0},{8,15},{9,14},{10,... | collective-permute-start | bytes 393224 | tf_op jit(solution)/shard_map/ppermute | solution.py:27
  24.9 0.4 shard_map.113
  25.3 0.7 collective-permute-done.16.refs_3_
  26.0 0.8 collective-permute-start.21
  26.7 5.8 %collective-permute-done.17.refs_4_ = bf16[4,128,128]{2,1,0:T(8,128)(2,1)S(1)} collective-permute-done((bf16[4,128,128]{2,1,0:T(8,128)(2,1)S(1)}, bf16[4,128,128]{2,1,0:T(8,128)(2,1)S(1)}, u32[]{:S(2)}, u32[]{:S(2)}) %collective-permute-start.17) | collective-permute-done | bytes 131104 | tf_op jit(solution)/shard_map/ppermute | solution.py:27
  32.5 1.8 %collective-permute-start.22 = (bf16[4,128,128]{2,1,0:T(8,128)(2,1)S(1)}, bf16[4,128,128]{2,1,0:T(8,128)(2,1)S(1)}, u32[]{:S(2)}, u32[]{:S(2)}) collective-permute-start(bf16[4,128,128]{2,1,0:T(8,128)(2,1)S(1)} %get-tuple-element.59), channel_id=1, source_target_pairs={{0,2},{1,3},{2,0},{3,1},{4,6},{5,7},{6,4},{7,5},{8,10},{9,11},{10,... | collective-permute-start | bytes 393224 | tf_op jit(solution)/shard_map/ppermute | solution.py:27
  34.3 1.6 %collective-permute-start.23 = (bf16[4,128,128]{2,1,0:T(8,128)(2,1)S(1)}, bf16[4,128,128]{2,1,0:T(8,128)(2,1)S(1)}, u32[]{:S(2)}, u32[]{:S(2)}) collective-permute-start(bf16[4,128,128]{2,1,0:T(8,128)(2,1)S(1)} %get-tuple-element.60), channel_id=1, source_target_pairs={{0,3},{1,2},{2,1},{3,0},{4,7},{5,6},{6,5},{7,4},{8,11},{9,10},{10,... | collective-permute-start | bytes 393224 | tf_op jit(solution)/shard_map/ppermute | solution.py:27
  35.9 0.3 collective-permute-start.24
  36.2 1.1 %collective-permute-start.25 = (bf16[4,128,128]{2,1,0:T(8,128)(2,1)S(1)}, bf16[4,128,128]{2,1,0:T(8,128)(2,1)S(1)}, u32[]{:S(2)}, u32[]{:S(2)}) collective-permute-start(bf16[4,128,128]{2,1,0:T(8,128)(2,1)S(1)} %get-tuple-element.62), channel_id=1, source_target_pairs={{0,5},{1,4},{2,7},{3,6},{4,1},{5,0},{6,3},{7,2},{8,13},{9,12},{10,... | collective-permute-start | bytes 393224 | tf_op jit(solution)/shard_map/ppermute | solution.py:27
  37.4 0.7 collective-permute-start
  38.1 1.6 %collective-permute-start.1 = (bf16[128,1024]{1,0:T(8,128)(2,1)S(1)}, bf16[128,1024]{1,0:T(8,128)(2,1)S(1)}, u32[]{:S(2)}, u32[]{:S(2)}) collective-permute-start(bf16[128,1024]{1,0:T(8,128)(2,1)S(1)} %copy-done.2), channel_id=1, source_target_pairs={{0,2},{1,3},{2,0},{3,1},{4,6},{5,7},{6,4},{7,5},{8,10},{9,11},{10,... | collective-permute-start | bytes 786440 | tf_op jit(solution)/shard_map/ppermute | solution.py:27
  39.6 0.5 collective-permute-done.23.refs_3_
  40.1 2.2 %collective-permute-done.24.refs_4_ = bf16[4,128,128]{2,1,0:T(8,128)(2,1)S(1)} collective-permute-done((bf16[4,128,128]{2,1,0:T(8,128)(2,1)S(1)}, bf16[4,128,128]{2,1,0:T(8,128)(2,1)S(1)}, u32[]{:S(2)}, u32[]{:S(2)}) %collective-permute-start.24) | collective-permute-done | bytes 131104 | tf_op jit(solution)/shard_map/ppermute | solution.py:27
  42.3 0.9 collective-permute-start.26
  43.1 0.2 collective-permute-done.25.refs_5_
  43.3 0.8 collective-permute-start.27
  44.1 5.8 %collective-permute-done.26.refs_6_ = bf16[4,128,128]{2,1,0:T(8,128)(2,1)S(1)} collective-permute-done((bf16[4,128,128]{2,1,0:T(8,128)(2,1)S(1)}, bf16[4,128,128]{2,1,0:T(8,128)(2,1)S(1)}, u32[]{:S(2)}, u32[]{:S(2)}) %collective-permute-start.26) | collective-permute-done | bytes 131104 | tf_op jit(solution)/shard_map/ppermute | solution.py:27
  49.9 2.7 %collective-permute-start.5 = (bf16[128,1024]{1,0:T(8,128)(2,1)S(1)}, bf16[128,1024]{1,0:T(8,128)(2,1)S(1)}, u32[]{:S(2)}, u32[]{:S(2)}) collective-permute-start(bf16[128,1024]{1,0:T(8,128)(2,1)S(1)} %copy-done.2), channel_id=1, source_target_pairs={{0,6},{1,7},{2,4},{3,5},{4,2},{5,3},{6,0},{7,1},{8,14},{9,15},{10,... | collective-permute-start | bytes 786440 | tf_op jit(solution)/shard_map/ppermute | solution.py:27
  52.6 0.5 collective-permute-start.40
  53.1 0.6 copy-done.9
  53.8 0.7 collective-permute-start.42
  54.5 1.8 %shard_map.115 = (bf16[8,128,128]{2,1,0:T(8,128)(2,1)S(1)}, bf16[8,128,128]{2,1,0:T(8,128)(2,1)S(1)}) custom-call(s32[18,32]{1,0:T(8,128)S(1)} %pad_add_fusion.list_ref, bf16[4,128,128]{2,1,0:T(8,128)(2,1)S(1)} %get-tuple-element.49.refs_0_, bf16[4,128,128]{2,1,0:T(8,128)(2,1)S(1)} %collective-permute-done.14.refs_1_, ...), custom_call_target="tpu_custom_call" | custom-call | bytes 1048576 | tf_op jit(solution)/shard_map/pallas_call | solution.py:43
  56.3 2.5 %collective-permute-start.44 = (bf16[1024,128]{1,0:T(8,128)(2,1)S(1)}, bf16[1024,128]{1,0:T(8,128)(2,1)S(1)}, u32[]{:S(2)}, u32[]{:S(2)}) collective-permute-start(bf16[1024,128]{1,0:T(8,128)(2,1)S(1)} %copy-done.6), channel_id=1, source_target_pairs={{0,6},{1,7},{2,4},{3,5},{4,2},{5,3},{6,0},{7,1},{8,14},{9,15},{10,... | collective-permute-start | bytes 786440 | tf_op jit(solution)/shard_map/ppermute | solution.py:27
  58.7 4.0 %collective-permute-done.3.refs_4_ = bf16[128,1024]{1,0:T(8,128)(2,1)S(1)} collective-permute-done((bf16[128,1024]{1,0:T(8,128)(2,1)S(1)}, bf16[128,1024]{1,0:T(8,128)(2,1)S(1)}, u32[]{:S(2)}, u32[]{:S(2)}) %collective-permute-start.3) | collective-permute-done | bytes 262176 | tf_op jit(solution)/shard_map/ppermute | solution.py:27
  62.8 1.6 %collective-permute-start.28 = (bf16[8,128,128]{2,1,0:T(8,128)(2,1)S(1)}, bf16[8,128,128]{2,1,0:T(8,128)(2,1)S(1)}, u32[]{:S(2)}, u32[]{:S(2)}) collective-permute-start(bf16[8,128,128]{2,1,0:T(8,128)(2,1)S(1)} %get-tuple-element.65), channel_id=1, source_target_pairs={{24,0},{0,8},{8,16},{16,24},{25,1},{1,9},{9,17},{17,25},{26,2},{2,... | collective-permute-start | bytes 786440 | tf_op jit(solution)/shard_map/ppermute | solution.py:22
  64.4 2.2 %collective-permute-start.29 = (bf16[8,128,128]{2,1,0:T(8,128)(2,1)S(1)}, bf16[8,128,128]{2,1,0:T(8,128)(2,1)S(1)}, u32[]{:S(2)}, u32[]{:S(2)}) collective-permute-start(bf16[8,128,128]{2,1,0:T(8,128)(2,1)S(1)} %get-tuple-element.66), channel_id=1, source_target_pairs={{8,0},{16,8},{24,16},{0,24},{9,1},{17,9},{25,17},{1,25},{10,2},{18... | collective-permute-start | bytes 786440 | tf_op jit(solution)/shard_map/ppermute | solution.py:22
  66.6 1.8 %shard_map.116 = (bf16[8,128,128]{2,1,0:T(8,128)(2,1)S(1)}, bf16[8,128,128]{2,1,0:T(8,128)(2,1)S(1)}) custom-call(s32[18,32]{1,0:T(8,128)S(1)} %pad_add_fusion.list_ref, bf16[4,128,128]{2,1,0:T(8,128)(2,1)S(1)} %get-tuple-element.57.refs_0_, bf16[4,128,128]{2,1,0:T(8,128)(2,1)S(1)} %collective-permute-done.21.refs_1_, ...), custom_call_target="tpu_custom_call" | custom-call | bytes 1048576 | tf_op jit(solution)/shard_map/pallas_call | solution.py:43
  68.5 3.8 %collective-permute-done.42.refs_12_ = bf16[1024,128]{1,0:T(8,128)(2,1)S(1)} collective-permute-done((bf16[1024,128]{1,0:T(8,128)(2,1)S(1)}, bf16[1024,128]{1,0:T(8,128)(2,1)S(1)}, u32[]{:S(2)}, u32[]{:S(2)}) %collective-permute-start.42) | collective-permute-done | bytes 262176 | tf_op jit(solution)/shard_map/ppermute | solution.py:27
  72.3 0.5 collective-permute-start.4
  72.8 1.1 %collective-permute-done.28.refs_0_ = bf16[8,128,128]{2,1,0:T(8,128)(2,1)S(1)} collective-permute-done((bf16[8,128,128]{2,1,0:T(8,128)(2,1)S(1)}, bf16[8,128,128]{2,1,0:T(8,128)(2,1)S(1)}, u32[]{:S(2)}, u32[]{:S(2)}) %collective-permute-start.28) | collective-permute-done | bytes 262176 | tf_op jit(solution)/shard_map/ppermute | solution.py:22
  73.9 4.3 %collective-permute-done.29.refs_1_ = bf16[8,128,128]{2,1,0:T(8,128)(2,1)S(1)} collective-permute-done((bf16[8,128,128]{2,1,0:T(8,128)(2,1)S(1)}, bf16[8,128,128]{2,1,0:T(8,128)(2,1)S(1)}, u32[]{:S(2)}, u32[]{:S(2)}) %collective-permute-start.29) | collective-permute-done | bytes 262176 | tf_op jit(solution)/shard_map/ppermute | solution.py:22
  78.1 2.3 %collective-permute-start.31 = (bf16[8,128,128]{2,1,0:T(8,128)(2,1)S(1)}, bf16[8,128,128]{2,1,0:T(8,128)(2,1)S(1)}, u32[]{:S(2)}, u32[]{:S(2)}) collective-permute-start(bf16[8,128,128]{2,1,0:T(8,128)(2,1)S(1)} %get-tuple-element.68), channel_id=1, source_target_pairs={{8,0},{16,8},{24,16},{0,24},{9,1},{17,9},{25,17},{1,25},{10,2},{18... | collective-permute-start | bytes 786440 | tf_op jit(solution)/shard_map/ppermute | solution.py:22
  80.4 1.4 %collective-permute-done.30.refs_2_ = bf16[8,128,128]{2,1,0:T(8,128)(2,1)S(1)} collective-permute-done((bf16[8,128,128]{2,1,0:T(8,128)(2,1)S(1)}, bf16[8,128,128]{2,1,0:T(8,128)(2,1)S(1)}, u32[]{:S(2)}, u32[]{:S(2)}) %collective-permute-start.30) | collective-permute-done | bytes 262176 | tf_op jit(solution)/shard_map/ppermute | solution.py:22
  81.8 0.5 collective-permute-start.41
  82.4 0.4 collective-permute-start.45
  82.8 1.4 %shard_map.112.key_ref = bf16[8,4,128,128]{3,2,1,0:T(8,128)(2,1)S(1)} custom-call(bf16[4,128,128]{2,1,0:T(8,128)(2,1)S(1)} %get-tuple-element.49.refs_0_, bf16[4,128,128]{2,1,0:T(8,128)(2,1)S(1)} %collective-permute-done.14.refs_1_, bf16[4,128,128]{2,1,0:T(8,128)(2,1)S(1)} %collective-permute-done.15.refs_2_, ...), custom_call_target="tpu_custom_call" | custom-call | bytes 2097152 | tf_op jit(solution)/shard_map/pallas_call | solution.py:43
  84.2 1.4 %shard_map.114.value_ref = bf16[8,4,128,128]{3,2,1,0:T(8,128)(2,1)S(1)} custom-call(bf16[4,128,128]{2,1,0:T(8,128)(2,1)S(1)} %get-tuple-element.57.refs_0_, bf16[4,128,128]{2,1,0:T(8,128)(2,1)S(1)} %collective-permute-done.21.refs_1_, bf16[4,128,128]{2,1,0:T(8,128)(2,1)S(1)} %collective-permute-done.22.refs_2_, ...), custom_call_target="tpu_custom_call" | custom-call | bytes 2097152 | tf_op jit(solution)/shard_map/pallas_call | solution.py:43
  85.7 1.3 %shard_map.110 = bf16[1024,384]{1,0:T(8,128)(2,1)S(1)} custom-call(bf16[128,1024]{1,0:T(8,128)(2,1)S(1)} %copy-done.2, bf16[128,1024]{1,0:T(8,128)(2,1)S(1)} %collective-permute-done.refs_1_, bf16[128,1024]{1,0:T(8,128)(2,1)S(1)} %collective-permute-done.1.refs_2_, bf16[128,1024]{1,0:T(8,128)(2,1)S(1)} %collective-permute-done.2.refs_3_, ...), custom_call_target="tpu_custom_call" | custom-call | flops 805306368 | bytes 2883584 | tf_op jit(solution)/shard_map/pallas_call | solution.py:43
  87.0 0.3 collective-permute-done.31.refs_3_
  87.3 3.1 %shard_map.117 = (bf16[128,128]{1,0:T(8,128)(2,1)S(1)}, bf16[128,128]{1,0:T(8,128)(2,1)S(1)}, bf16[128,128]{1,0:T(8,128)(2,1)S(1)}, bf16[128,128]{1,0:T(8,128)(2...) custom-call(s32[18,32]{1,0:T(8,128)S(1)} %pad_add_fusion.list_ref, ...), custom_call_target="tpu_custom_call" | custom-call | flops 603979776 | bytes 2097152 | tf_op jit(solution)/shard_map/pallas_call | solution.py:43
  90.5 2.4 %collective-permute-start.33 = (bf16[128,128]{1,0:T(8,128)(2,1)S(1)}, bf16[128,128]{1,0:T(8,128)(2,1)S(1)}, u32[]{:S(2)}, u32[]{:S(2)}) collective-permute-start(bf16[128,128]{1,0:T(8,128)(2,1)S(1)} %get-tuple-element.71), channel_id=1, source_target_pairs={{0,2},{1,3},{2,0},{3,1},{4,6},{5,7},{6,4},{7,5},{8,10},{9,11},{10,... | collective-permute-start | bytes 98312 | tf_op jit(solution)/shard_map/ppermute | solution.py:27
  92.9 1.5 %collective-permute-start.36 = (bf16[128,128]{1,0:T(8,128)(2,1)S(1)}, bf16[128,128]{1,0:T(8,128)(2,1)S(1)}, u32[]{:S(2)}, u32[]{:S(2)}) collective-permute-start(bf16[128,128]{1,0:T(8,128)(2,1)S(1)} %get-tuple-element.74), channel_id=1, source_target_pairs={{0,5},{1,4},{2,7},{3,6},{4,1},{5,0},{6,3},{7,2},{8,13},{9,12},{10,... | collective-permute-start | bytes 98312 | tf_op jit(solution)/shard_map/ppermute | solution.py:27
  94.4 1.7 %collective-permute-start.37 = (bf16[128,128]{1,0:T(8,128)(2,1)S(1)}, bf16[128,128]{1,0:T(8,128)(2,1)S(1)}, u32[]{:S(2)}, u32[]{:S(2)}) collective-permute-start(bf16[128,128]{1,0:T(8,128)(2,1)S(1)} %get-tuple-element.75), channel_id=1, source_target_pairs={{0,6},{1,7},{2,4},{3,5},{4,2},{5,3},{6,0},{7,1},{8,14},{9,15},{10,... | collective-permute-start | bytes 98312 | tf_op jit(solution)/shard_map/ppermute | solution.py:27
  96.1 1.2 %collective-permute-start.38 = (bf16[128,128]{1,0:T(8,128)(2,1)S(1)}, bf16[128,128]{1,0:T(8,128)(2,1)S(1)}, u32[]{:S(2)}, u32[]{:S(2)}) collective-permute-start(bf16[128,128]{1,0:T(8,128)(2,1)S(1)} %get-tuple-element.76), channel_id=1, source_target_pairs={{0,7},{1,6},{2,5},{3,4},{4,3},{5,2},{6,1},{7,0},{8,15},{9,14},{10,... | collective-permute-start | bytes 98312 | tf_op jit(solution)/shard_map/ppermute | solution.py:27
  97.3 1.9 %collective-permute-done.37.refs_6_ = bf16[128,128]{1,0:T(8,128)(2,1)S(1)} collective-permute-done((bf16[128,128]{1,0:T(8,128)(2,1)S(1)}, bf16[128,128]{1,0:T(8,128)(2,1)S(1)}, u32[]{:S(2)}, u32[]{:S(2)}) %collective-permute-start.37) | collective-permute-done | bytes 32800 | tf_op jit(solution)/shard_map/ppermute | solution.py:27
  99.3 1.4 %collective-permute-done.38.refs_7_ = bf16[128,128]{1,0:T(8,128)(2,1)S(1)} collective-permute-done((bf16[128,128]{1,0:T(8,128)(2,1)S(1)}, bf16[128,128]{1,0:T(8,128)(2,1)S(1)}, u32[]{:S(2)}, u32[]{:S(2)}) %collective-permute-start.38) | collective-permute-done | bytes 32800 | tf_op jit(solution)/shard_map/ppermute | solution.py:27
  100.7 1.3 %shard_map.118 = bf16[128,1024]{1,0:T(8,128)(2,1)} custom-call(bf16[128,128]{1,0:T(8,128)(2,1)S(1)} %get-tuple-element.69.refs_0_, bf16[128,128]{1,0:T(8,128)(2,1)S(1)} %collective-permute-done.32.refs_1_, bf16[128,128]{1,0:T(8,128)(2,1)S(1)} %collective-permute-done.33.refs_2_, bf16[128,128]{1,0:T(8,128)(2,1)S(1)} %collective-permute-done.34.refs_3_, ...), custom_call_target="tpu_custom_call" | custom-call | flops 268435456 | bytes 2097152 | tf_op jit(solution)/shard_map/pallas_call | solution.py:43
  (61 shorter events, 0.5 us)
Async XLA Ops:
  0.0 0.9 copy-start.3
  1.0 0.9 copy-start.4
  1.9 0.9 copy-start.5
  3.4 6.7 %collective-permute-start.7 = (bf16[128,384]{1,0:T(8,128)(2,1)S(1)}, bf16[128,384]{1,0:T(8,128)(2,1)S(1)}, u32[]{:S(2)}, u32[]{:S(2)}) collective-permute-start(bf16[128,384]{1,0:T(8,128)(2,1)S(1)} %get-tuple-element.42), channel_id=1, source_target_pairs={{0,1},{1,0},{2,3},{3,2},{4,5},{5,4},{6,7},{7,6},{8,9},{9,8},{10,11... | collective-permute-start | bytes 294920 | tf_op jit(solution)/shard_map/ppermute | solution.py:27
  3.9 7.6 %collective-permute-start.8 = (bf16[128,384]{1,0:T(8,128)(2,1)S(1)}, bf16[128,384]{1,0:T(8,128)(2,1)S(1)}, u32[]{:S(2)}, u32[]{:S(2)}) collective-permute-start(bf16[128,384]{1,0:T(8,128)(2,1)S(1)} %get-tuple-element.43), channel_id=1, source_target_pairs={{0,2},{1,3},{2,0},{3,1},{4,6},{5,7},{6,4},{7,5},{8,10},{9,11},{10,... | collective-permute-start | bytes 294920 | tf_op jit(solution)/shard_map/ppermute | solution.py:27
  6.5 5.3 %collective-permute-start.9 = (bf16[128,384]{1,0:T(8,128)(2,1)S(1)}, bf16[128,384]{1,0:T(8,128)(2,1)S(1)}, u32[]{:S(2)}, u32[]{:S(2)}) collective-permute-start(bf16[128,384]{1,0:T(8,128)(2,1)S(1)} %get-tuple-element.44), channel_id=1, source_target_pairs={{0,3},{1,2},{2,1},{3,0},{4,7},{5,6},{6,5},{7,4},{8,11},{9,10},{10,... | collective-permute-start | bytes 294920 | tf_op jit(solution)/shard_map/ppermute | solution.py:27
  6.5 7.6 %collective-permute-start.10 = (bf16[128,384]{1,0:T(8,128)(2,1)S(1)}, bf16[128,384]{1,0:T(8,128)(2,1)S(1)}, u32[]{:S(2)}, u32[]{:S(2)}) collective-permute-start(bf16[128,384]{1,0:T(8,128)(2,1)S(1)} %get-tuple-element.45), channel_id=1, source_target_pairs={{0,4},{1,5},{2,6},{3,7},{4,0},{5,1},{6,2},{7,3},{8,12},{9,13},{10,... | collective-permute-start | bytes 294920 | tf_op jit(solution)/shard_map/ppermute | solution.py:27
  8.3 1.2 %copy-start = (bf16[4,128,1024]{2,1,0:T(8,128)(2,1)S(1)}, bf16[4,128,1024]{2,1,0:T(8,128)(2,1)}, u32[]{:S(2)}) copy-start(bf16[4,128,1024]{2,1,0:T(8,128)(2,1)} %refs_0_.6) | copy-start | bytes 3145732
  9.5 15.4 %copy-start.1 = (bf16[4,128,1024]{2,1,0:T(8,128)(2,1)S(1)}, bf16[4,128,1024]{2,1,0:T(8,128)(2,1)}, u32[]{:S(2)}) copy-start(bf16[4,128,1024]{2,1,0:T(8,128)(2,1)} %refs_0_.7) | copy-start | bytes 3145732
  9.9 12.1 %collective-permute-start.14 = (bf16[4,128,128]{2,1,0:T(8,128)(2,1)S(1)}, bf16[4,128,128]{2,1,0:T(8,128)(2,1)S(1)}, u32[]{:S(2)}, u32[]{:S(2)}) collective-permute-start(bf16[4,128,128]{2,1,0:T(8,128)(2,1)S(1)} %get-tuple-element.50), channel_id=1, source_target_pairs={{0,1},{1,0},{2,3},{3,2},{4,5},{5,4},{6,7},{7,6},{8,9},{9,8},{10,11... | collective-permute-start | bytes 393224 | tf_op jit(solution)/shard_map/ppermute | solution.py:27
  10.0 13.8 %collective-permute-start.15 = (bf16[4,128,128]{2,1,0:T(8,128)(2,1)S(1)}, bf16[4,128,128]{2,1,0:T(8,128)(2,1)S(1)}, u32[]{:S(2)}, u32[]{:S(2)}) collective-permute-start(bf16[4,128,128]{2,1,0:T(8,128)(2,1)S(1)} %get-tuple-element.51), channel_id=1, source_target_pairs={{0,2},{1,3},{2,0},{3,1},{4,6},{5,7},{6,4},{7,5},{8,10},{9,11},{10,... | collective-permute-start | bytes 393224 | tf_op jit(solution)/shard_map/ppermute | solution.py:27
  11.5 9.0 %collective-permute-start.11 = (bf16[128,384]{1,0:T(8,128)(2,1)S(1)}, bf16[128,384]{1,0:T(8,128)(2,1)S(1)}, u32[]{:S(2)}, u32[]{:S(2)}) collective-permute-start(bf16[128,384]{1,0:T(8,128)(2,1)S(1)} %get-tuple-element.46), channel_id=1, source_target_pairs={{0,5},{1,4},{2,7},{3,6},{4,1},{5,0},{6,3},{7,2},{8,13},{9,12},{10,... | collective-permute-start | bytes 294920 | tf_op jit(solution)/shard_map/ppermute | solution.py:27
  11.8 8.7 %collective-permute-start.12 = (bf16[128,384]{1,0:T(8,128)(2,1)S(1)}, bf16[128,384]{1,0:T(8,128)(2,1)S(1)}, u32[]{:S(2)}, u32[]{:S(2)}) collective-permute-start(bf16[128,384]{1,0:T(8,128)(2,1)S(1)} %get-tuple-element.47), channel_id=1, source_target_pairs={{0,6},{1,7},{2,4},{3,5},{4,2},{5,3},{6,0},{7,1},{8,14},{9,15},{10,... | collective-permute-start | bytes 294920 | tf_op jit(solution)/shard_map/ppermute | solution.py:27
  14.1 6.4 %collective-permute-start.13 = (bf16[128,384]{1,0:T(8,128)(2,1)S(1)}, bf16[128,384]{1,0:T(8,128)(2,1)S(1)}, u32[]{:S(2)}, u32[]{:S(2)}) collective-permute-start(bf16[128,384]{1,0:T(8,128)(2,1)S(1)} %get-tuple-element.48), channel_id=1, source_target_pairs={{0,7},{1,6},{2,5},{3,4},{4,3},{5,2},{6,1},{7,0},{8,15},{9,14},{10,... | collective-permute-start | bytes 294920 | tf_op jit(solution)/shard_map/ppermute | solution.py:27
  20.5 5.5 %collective-permute-start.16 = (bf16[4,128,128]{2,1,0:T(8,128)(2,1)S(1)}, bf16[4,128,128]{2,1,0:T(8,128)(2,1)S(1)}, u32[]{:S(2)}, u32[]{:S(2)}) collective-permute-start(bf16[4,128,128]{2,1,0:T(8,128)(2,1)S(1)} %get-tuple-element.52), channel_id=1, source_target_pairs={{0,3},{1,2},{2,1},{3,0},{4,7},{5,6},{6,5},{7,4},{8,11},{9,10},{10,... | collective-permute-start | bytes 393224 | tf_op jit(solution)/shard_map/ppermute | solution.py:27
  20.5 12.0 %collective-permute-start.17 = (bf16[4,128,128]{2,1,0:T(8,128)(2,1)S(1)}, bf16[4,128,128]{2,1,0:T(8,128)(2,1)S(1)}, u32[]{:S(2)}, u32[]{:S(2)}) collective-permute-start(bf16[4,128,128]{2,1,0:T(8,128)(2,1)S(1)} %get-tuple-element.53), channel_id=1, source_target_pairs={{0,4},{1,5},{2,6},{3,7},{4,0},{5,1},{6,2},{7,3},{8,12},{9,13},{10,... | collective-permute-start | bytes 393224 | tf_op jit(solution)/shard_map/ppermute | solution.py:27
  20.5 13.7 %collective-permute-start.18 = (bf16[4,128,128]{2,1,0:T(8,128)(2,1)S(1)}, bf16[4,128,128]{2,1,0:T(8,128)(2,1)S(1)}, u32[]{:S(2)}, u32[]{:S(2)}) collective-permute-start(bf16[4,128,128]{2,1,0:T(8,128)(2,1)S(1)} %get-tuple-element.54), channel_id=1, source_target_pairs={{0,5},{1,4},{2,7},{3,6},{4,1},{5,0},{6,3},{7,2},{8,13},{9,12},{10,... | collective-permute-start | bytes 393224 | tf_op jit(solution)/shard_map/ppermute | solution.py:27
  22.0 13.9 %collective-permute-start.19 = (bf16[4,128,128]{2,1,0:T(8,128)(2,1)S(1)}, bf16[4,128,128]{2,1,0:T(8,128)(2,1)S(1)}, u32[]{:S(2)}, u32[]{:S(2)}) collective-permute-start(bf16[4,128,128]{2,1,0:T(8,128)(2,1)S(1)} %get-tuple-element.55), channel_id=1, source_target_pairs={{0,6},{1,7},{2,4},{3,5},{4,2},{5,3},{6,0},{7,1},{8,14},{9,15},{10,... | collective-permute-start | bytes 393224 | tf_op jit(solution)/shard_map/ppermute | solution.py:27
  23.8 13.5 %copy-start.2 = (bf16[128,1024]{1,0:T(8,128)(2,1)S(1)}, bf16[128,1024]{1,0:T(8,128)(2,1)}, u32[]{:S(2)}) copy-start(bf16[128,1024]{1,0:T(8,128)(2,1)} %refs_0_.5) | copy-start | bytes 786436
  23.8 28.8 %copy-start.6 = (bf16[1024,128]{1,0:T(8,128)(2,1)S(1)}, bf16[1024,128]{1,0:T(8,128)(2,1)}, u32[]{:S(2)}) copy-start(bf16[1024,128]{1,0:T(8,128)(2,1)} %refs_8_.1) | copy-start | bytes 786436
  23.8 12.4 %collective-permute-start.20 = (bf16[4,128,128]{2,1,0:T(8,128)(2,1)S(1)}, bf16[4,128,128]{2,1,0:T(8,128)(2,1)S(1)}, u32[]{:S(2)}, u32[]{:S(2)}) collective-permute-start(bf16[4,128,128]{2,1,0:T(8,128)(2,1)S(1)} %get-tuple-element.56), channel_id=1, source_target_pairs={{0,7},{1,6},{2,5},{3,4},{4,3},{5,2},{6,1},{7,0},{8,15},{9,14},{10,... | collective-permute-start | bytes 393224 | tf_op jit(solution)/shard_map/ppermute | solution.py:27
  26.0 11.4 %collective-permute-start.21 = (bf16[4,128,128]{2,1,0:T(8,128)(2,1)S(1)}, bf16[4,128,128]{2,1,0:T(8,128)(2,1)S(1)}, u32[]{:S(2)}, u32[]{:S(2)}) collective-permute-start(bf16[4,128,128]{2,1,0:T(8,128)(2,1)S(1)} %get-tuple-element.58), channel_id=1, source_target_pairs={{0,1},{1,0},{2,3},{3,2},{4,5},{5,4},{6,7},{7,6},{8,9},{9,8},{10,11... | collective-permute-start | bytes 393224 | tf_op jit(solution)/shard_map/ppermute | solution.py:27
  32.5 5.6 %collective-permute-start.22 = (bf16[4,128,128]{2,1,0:T(8,128)(2,1)S(1)}, bf16[4,128,128]{2,1,0:T(8,128)(2,1)S(1)}, u32[]{:S(2)}, u32[]{:S(2)}) collective-permute-start(bf16[4,128,128]{2,1,0:T(8,128)(2,1)S(1)} %get-tuple-element.59), channel_id=1, source_target_pairs={{0,2},{1,3},{2,0},{3,1},{4,6},{5,7},{6,4},{7,5},{8,10},{9,11},{10,... | collective-permute-start | bytes 393224 | tf_op jit(solution)/shard_map/ppermute | solution.py:27
  34.3 5.8 %collective-permute-start.23 = (bf16[4,128,128]{2,1,0:T(8,128)(2,1)S(1)}, bf16[4,128,128]{2,1,0:T(8,128)(2,1)S(1)}, u32[]{:S(2)}, u32[]{:S(2)}) collective-permute-start(bf16[4,128,128]{2,1,0:T(8,128)(2,1)S(1)} %get-tuple-element.60), channel_id=1, source_target_pairs={{0,3},{1,2},{2,1},{3,0},{4,7},{5,6},{6,5},{7,4},{8,11},{9,10},{10,... | collective-permute-start | bytes 393224 | tf_op jit(solution)/shard_map/ppermute | solution.py:27
  35.9 6.4 %collective-permute-start.24 = (bf16[4,128,128]{2,1,0:T(8,128)(2,1)S(1)}, bf16[4,128,128]{2,1,0:T(8,128)(2,1)S(1)}, u32[]{:S(2)}, u32[]{:S(2)}) collective-permute-start(bf16[4,128,128]{2,1,0:T(8,128)(2,1)S(1)} %get-tuple-element.61), channel_id=1, source_target_pairs={{0,4},{1,5},{2,6},{3,7},{4,0},{5,1},{6,2},{7,3},{8,12},{9,13},{10,... | collective-permute-start | bytes 393224 | tf_op jit(solution)/shard_map/ppermute | solution.py:27
  36.2 7.1 %collective-permute-start.25 = (bf16[4,128,128]{2,1,0:T(8,128)(2,1)S(1)}, bf16[4,128,128]{2,1,0:T(8,128)(2,1)S(1)}, u32[]{:S(2)}, u32[]{:S(2)}) collective-permute-start(bf16[4,128,128]{2,1,0:T(8,128)(2,1)S(1)} %get-tuple-element.62), channel_id=1, source_target_pairs={{0,5},{1,4},{2,7},{3,6},{4,1},{5,0},{6,3},{7,2},{8,13},{9,12},{10,... | collective-permute-start | bytes 393224 | tf_op jit(solution)/shard_map/ppermute | solution.py:27
  37.4 16.4 %collective-permute-start = (bf16[128,1024]{1,0:T(8,128)(2,1)S(1)}, bf16[128,1024]{1,0:T(8,128)(2,1)S(1)}, u32[]{:S(2)}, u32[]{:S(2)}) collective-permute-start(bf16[128,1024]{1,0:T(8,128)(2,1)S(1)} %copy-done.2), channel_id=1, source_target_pairs={{0,1},{1,0},{2,3},{3,2},{4,5},{5,4},{6,7},{7,6},{8,9},{9,8},{10,11... | collective-permute-start | bytes 786440 | tf_op jit(solution)/shard_map/ppermute | solution.py:27
  38.1 18.2 %collective-permute-start.1 = (bf16[128,1024]{1,0:T(8,128)(2,1)S(1)}, bf16[128,1024]{1,0:T(8,128)(2,1)S(1)}, u32[]{:S(2)}, u32[]{:S(2)}) collective-permute-start(bf16[128,1024]{1,0:T(8,128)(2,1)S(1)} %copy-done.2), channel_id=1, source_target_pairs={{0,2},{1,3},{2,0},{3,1},{4,6},{5,7},{6,4},{7,5},{8,10},{9,11},{10,... | collective-permute-start | bytes 786440 | tf_op jit(solution)/shard_map/ppermute | solution.py:27
  40.1 22.7 %collective-permute-start.3 = (bf16[128,1024]{1,0:T(8,128)(2,1)S(1)}, bf16[128,1024]{1,0:T(8,128)(2,1)S(1)}, u32[]{:S(2)}, u32[]{:S(2)}) collective-permute-start(bf16[128,1024]{1,0:T(8,128)(2,1)S(1)} %copy-done.2), channel_id=1, source_target_pairs={{0,4},{1,5},{2,6},{3,7},{4,0},{5,1},{6,2},{7,3},{8,12},{9,13},{10,... | collective-permute-start | bytes 786440 | tf_op jit(solution)/shard_map/ppermute | solution.py:27
  42.3 7.6 %collective-permute-start.26 = (bf16[4,128,128]{2,1,0:T(8,128)(2,1)S(1)}, bf16[4,128,128]{2,1,0:T(8,128)(2,1)S(1)}, u32[]{:S(2)}, u32[]{:S(2)}) collective-permute-start(bf16[4,128,128]{2,1,0:T(8,128)(2,1)S(1)} %get-tuple-element.63), channel_id=1, source_target_pairs={{0,6},{1,7},{2,4},{3,5},{4,2},{5,3},{6,0},{7,1},{8,14},{9,15},{10,... | collective-permute-start | bytes 393224 | tf_op jit(solution)/shard_map/ppermute | solution.py:27
  43.3 9.8 %copy-start.8 = (s32[32,8]{0,1:T(8,128)S(1)}, s32[32,8]{0,1:T(8,128)}, u32[]{:S(2)}) copy-start(s32[32,8]{0,1:T(8,128)} %param.18) | copy-start | bytes 3076
  43.3 9.8 %copy-start.7 = (s32[32,8]{0,1:T(8,128)S(1)}, s32[32,8]{0,1:T(8,128)}, u32[]{:S(2)}) copy-start(s32[32,8]{0,1:T(8,128)} %param.19) | copy-start | bytes 3076
  43.3 9.3 %collective-permute-start.27 = (bf16[4,128,128]{2,1,0:T(8,128)(2,1)S(1)}, bf16[4,128,128]{2,1,0:T(8,128)(2,1)S(1)}, u32[]{:S(2)}, u32[]{:S(2)}) collective-permute-start(bf16[4,128,128]{2,1,0:T(8,128)(2,1)S(1)} %get-tuple-element.64), channel_id=1, source_target_pairs={{0,7},{1,6},{2,5},{3,4},{4,3},{5,2},{6,1},{7,0},{8,15},{9,14},{10,... | collective-permute-start | bytes 393224 | tf_op jit(solution)/shard_map/ppermute | solution.py:27
  49.9 14.5 %collective-permute-start.5 = (bf16[128,1024]{1,0:T(8,128)(2,1)S(1)}, bf16[128,1024]{1,0:T(8,128)(2,1)S(1)}, u32[]{:S(2)}, u32[]{:S(2)}) collective-permute-start(bf16[128,1024]{1,0:T(8,128)(2,1)S(1)} %copy-done.2), channel_id=1, source_target_pairs={{0,6},{1,7},{2,4},{3,5},{4,2},{5,3},{6,0},{7,1},{8,14},{9,15},{10,... | collective-permute-start | bytes 786440 | tf_op jit(solution)/shard_map/ppermute | solution.py:27
  52.6 15.8 %collective-permute-start.40 = (bf16[1024,128]{1,0:T(8,128)(2,1)S(1)}, bf16[1024,128]{1,0:T(8,128)(2,1)S(1)}, u32[]{:S(2)}, u32[]{:S(2)}) collective-permute-start(bf16[1024,128]{1,0:T(8,128)(2,1)S(1)} %copy-done.6), channel_id=1, source_target_pairs={{0,2},{1,3},{2,0},{3,1},{4,6},{5,7},{6,4},{7,5},{8,10},{9,11},{10,... | collective-permute-start | bytes 786440 | tf_op jit(solution)/shard_map/ppermute | solution.py:27
  53.1 0.7 copy-start.9
  53.1 0.7 copy-start.10
  53.8 18.5 %collective-permute-start.42 = (bf16[1024,128]{1,0:T(8,128)(2,1)S(1)}, bf16[1024,128]{1,0:T(8,128)(2,1)S(1)}, u32[]{:S(2)}, u32[]{:S(2)}) collective-permute-start(bf16[1024,128]{1,0:T(8,128)(2,1)S(1)} %copy-done.6), channel_id=1, source_target_pairs={{0,4},{1,5},{2,6},{3,7},{4,0},{5,1},{6,2},{7,3},{8,12},{9,13},{10,... | collective-permute-start | bytes 786440 | tf_op jit(solution)/shard_map/ppermute | solution.py:27
  56.3 16.0 %collective-permute-start.44 = (bf16[1024,128]{1,0:T(8,128)(2,1)S(1)}, bf16[1024,128]{1,0:T(8,128)(2,1)S(1)}, u32[]{:S(2)}, u32[]{:S(2)}) collective-permute-start(bf16[1024,128]{1,0:T(8,128)(2,1)S(1)} %copy-done.6), channel_id=1, source_target_pairs={{0,6},{1,7},{2,4},{3,5},{4,2},{5,3},{6,0},{7,1},{8,14},{9,15},{10,... | collective-permute-start | bytes 786440 | tf_op jit(solution)/shard_map/ppermute | solution.py:27
  62.8 11.1 %collective-permute-start.28 = (bf16[8,128,128]{2,1,0:T(8,128)(2,1)S(1)}, bf16[8,128,128]{2,1,0:T(8,128)(2,1)S(1)}, u32[]{:S(2)}, u32[]{:S(2)}) collective-permute-start(bf16[8,128,128]{2,1,0:T(8,128)(2,1)S(1)} %get-tuple-element.65), channel_id=1, source_target_pairs={{24,0},{0,8},{8,16},{16,24},{25,1},{1,9},{9,17},{17,25},{26,2},{2,... | collective-permute-start | bytes 786440 | tf_op jit(solution)/shard_map/ppermute | solution.py:22
  64.4 13.8 %collective-permute-start.29 = (bf16[8,128,128]{2,1,0:T(8,128)(2,1)S(1)}, bf16[8,128,128]{2,1,0:T(8,128)(2,1)S(1)}, u32[]{:S(2)}, u32[]{:S(2)}) collective-permute-start(bf16[8,128,128]{2,1,0:T(8,128)(2,1)S(1)} %get-tuple-element.66), channel_id=1, source_target_pairs={{8,0},{16,8},{24,16},{0,24},{9,1},{17,9},{25,17},{1,25},{10,2},{18... | collective-permute-start | bytes 786440 | tf_op jit(solution)/shard_map/ppermute | solution.py:22
  68.4 13.3 %collective-permute-start.30 = (bf16[8,128,128]{2,1,0:T(8,128)(2,1)S(1)}, bf16[8,128,128]{2,1,0:T(8,128)(2,1)S(1)}, u32[]{:S(2)}, u32[]{:S(2)}) collective-permute-start(bf16[8,128,128]{2,1,0:T(8,128)(2,1)S(1)} %get-tuple-element.67), channel_id=1, source_target_pairs={{24,0},{0,8},{8,16},{16,24},{25,1},{1,9},{9,17},{17,25},{26,2},{2,... | collective-permute-start | bytes 786440 | tf_op jit(solution)/shard_map/ppermute | solution.py:22
  72.3 9.5 %collective-permute-start.2 = (bf16[128,1024]{1,0:T(8,128)(2,1)S(1)}, bf16[128,1024]{1,0:T(8,128)(2,1)S(1)}, u32[]{:S(2)}, u32[]{:S(2)}) collective-permute-start(bf16[128,1024]{1,0:T(8,128)(2,1)S(1)} %collective-permute-done.1.refs_2_), channel_id=1, source_target_pairs={{0,1},{1,0},{2,3},{3,2},{4,5},{5,4},{6,7},{7,6},{8,9},{9,8},{10,11... | collective-permute-start | bytes 786440 | tf_op jit(solution)/shard_map/ppermute | solution.py:27
  72.3 10.0 %collective-permute-start.4 = (bf16[128,1024]{1,0:T(8,128)(2,1)S(1)}, bf16[128,1024]{1,0:T(8,128)(2,1)S(1)}, u32[]{:S(2)}, u32[]{:S(2)}) collective-permute-start(bf16[128,1024]{1,0:T(8,128)(2,1)S(1)} %collective-permute-done.3.refs_4_), channel_id=1, source_target_pairs={{0,1},{1,0},{2,3},{3,2},{4,5},{5,4},{6,7},{7,6},{8,9},{9,8},{10,11... | collective-permute-start | bytes 786440 | tf_op jit(solution)/shard_map/ppermute | solution.py:27
  73.9 8.5 %collective-permute-start.6 = (bf16[128,1024]{1,0:T(8,128)(2,1)S(1)}, bf16[128,1024]{1,0:T(8,128)(2,1)S(1)}, u32[]{:S(2)}, u32[]{:S(2)}) collective-permute-start(bf16[128,1024]{1,0:T(8,128)(2,1)S(1)} %collective-permute-done.5.refs_6_), channel_id=1, source_target_pairs={{0,1},{1,0},{2,3},{3,2},{4,5},{5,4},{6,7},{7,6},{8,9},{9,8},{10,11... | collective-permute-start | bytes 786440 | tf_op jit(solution)/shard_map/ppermute | solution.py:27
  78.1 9.2 %collective-permute-start.31 = (bf16[8,128,128]{2,1,0:T(8,128)(2,1)S(1)}, bf16[8,128,128]{2,1,0:T(8,128)(2,1)S(1)}, u32[]{:S(2)}, u32[]{:S(2)}) collective-permute-start(bf16[8,128,128]{2,1,0:T(8,128)(2,1)S(1)} %get-tuple-element.68), channel_id=1, source_target_pairs={{8,0},{16,8},{24,16},{0,24},{9,1},{17,9},{25,17},{1,25},{10,2},{18... | collective-permute-start | bytes 786440 | tf_op jit(solution)/shard_map/ppermute | solution.py:22
  81.8 8.7 %collective-permute-start.39 = (bf16[1024,128]{1,0:T(8,128)(2,1)S(1)}, bf16[1024,128]{1,0:T(8,128)(2,1)S(1)}, u32[]{:S(2)}, u32[]{:S(2)}) collective-permute-start(bf16[1024,128]{1,0:T(8,128)(2,1)S(1)} %copy-done.6), channel_id=1, source_target_pairs={{0,1},{1,0},{2,3},{3,2},{4,5},{5,4},{6,7},{7,6},{8,9},{9,8},{10,11... | collective-permute-start | bytes 786440 | tf_op jit(solution)/shard_map/ppermute | solution.py:27
  81.8 11.0 %collective-permute-start.41 = (bf16[1024,128]{1,0:T(8,128)(2,1)S(1)}, bf16[1024,128]{1,0:T(8,128)(2,1)S(1)}, u32[]{:S(2)}, u32[]{:S(2)}) collective-permute-start(bf16[1024,128]{1,0:T(8,128)(2,1)S(1)} %collective-permute-done.40.refs_10_), channel_id=1, source_target_pairs={{0,1},{1,0},{2,3},{3,2},{4,5},{5,4},{6,7},{7,6},{8,9},{9,8},{10,11... | collective-permute-start | bytes 786440 | tf_op jit(solution)/shard_map/ppermute | solution.py:27
  82.3 10.6 %collective-permute-start.43 = (bf16[1024,128]{1,0:T(8,128)(2,1)S(1)}, bf16[1024,128]{1,0:T(8,128)(2,1)S(1)}, u32[]{:S(2)}, u32[]{:S(2)}) collective-permute-start(bf16[1024,128]{1,0:T(8,128)(2,1)S(1)} %collective-permute-done.42.refs_12_), channel_id=1, source_target_pairs={{0,1},{1,0},{2,3},{3,2},{4,5},{5,4},{6,7},{7,6},{8,9},{9,8},{10,11... | collective-permute-start | bytes 786440 | tf_op jit(solution)/shard_map/ppermute | solution.py:27
  82.4 10.6 %collective-permute-start.45 = (bf16[1024,128]{1,0:T(8,128)(2,1)S(1)}, bf16[1024,128]{1,0:T(8,128)(2,1)S(1)}, u32[]{:S(2)}, u32[]{:S(2)}) collective-permute-start(bf16[1024,128]{1,0:T(8,128)(2,1)S(1)} %collective-permute-done.44.refs_14_), channel_id=1, source_target_pairs={{0,1},{1,0},{2,3},{3,2},{4,5},{5,4},{6,7},{7,6},{8,9},{9,8},{10,11... | collective-permute-start | bytes 786440 | tf_op jit(solution)/shard_map/ppermute | solution.py:27
  90.4 4.0 %collective-permute-start.32 = (bf16[128,128]{1,0:T(8,128)(2,1)S(1)}, bf16[128,128]{1,0:T(8,128)(2,1)S(1)}, u32[]{:S(2)}, u32[]{:S(2)}) collective-permute-start(bf16[128,128]{1,0:T(8,128)(2,1)S(1)} %get-tuple-element.70), channel_id=1, source_target_pairs={{0,1},{1,0},{2,3},{3,2},{4,5},{5,4},{6,7},{7,6},{8,9},{9,8},{10,11... | collective-permute-start | bytes 98312 | tf_op jit(solution)/shard_map/ppermute | solution.py:27
  90.5 5.7 %collective-permute-start.33 = (bf16[128,128]{1,0:T(8,128)(2,1)S(1)}, bf16[128,128]{1,0:T(8,128)(2,1)S(1)}, u32[]{:S(2)}, u32[]{:S(2)}) collective-permute-start(bf16[128,128]{1,0:T(8,128)(2,1)S(1)} %get-tuple-element.71), channel_id=1, source_target_pairs={{0,2},{1,3},{2,0},{3,1},{4,6},{5,7},{6,4},{7,5},{8,10},{9,11},{10,... | collective-permute-start | bytes 98312 | tf_op jit(solution)/shard_map/ppermute | solution.py:27
  92.8 4.5 %collective-permute-start.34 = (bf16[128,128]{1,0:T(8,128)(2,1)S(1)}, bf16[128,128]{1,0:T(8,128)(2,1)S(1)}, u32[]{:S(2)}, u32[]{:S(2)}) collective-permute-start(bf16[128,128]{1,0:T(8,128)(2,1)S(1)} %get-tuple-element.72), channel_id=1, source_target_pairs={{0,3},{1,2},{2,1},{3,0},{4,7},{5,6},{6,5},{7,4},{8,11},{9,10},{10,... | collective-permute-start | bytes 98312 | tf_op jit(solution)/shard_map/ppermute | solution.py:27
  92.9 4.4 %collective-permute-start.35 = (bf16[128,128]{1,0:T(8,128)(2,1)S(1)}, bf16[128,128]{1,0:T(8,128)(2,1)S(1)}, u32[]{:S(2)}, u32[]{:S(2)}) collective-permute-start(bf16[128,128]{1,0:T(8,128)(2,1)S(1)} %get-tuple-element.73), channel_id=1, source_target_pairs={{0,4},{1,5},{2,6},{3,7},{4,0},{5,1},{6,2},{7,3},{8,12},{9,13},{10,... | collective-permute-start | bytes 98312 | tf_op jit(solution)/shard_map/ppermute | solution.py:27
  92.9 4.4 %collective-permute-start.36 = (bf16[128,128]{1,0:T(8,128)(2,1)S(1)}, bf16[128,128]{1,0:T(8,128)(2,1)S(1)}, u32[]{:S(2)}, u32[]{:S(2)}) collective-permute-start(bf16[128,128]{1,0:T(8,128)(2,1)S(1)} %get-tuple-element.74), channel_id=1, source_target_pairs={{0,5},{1,4},{2,7},{3,6},{4,1},{5,0},{6,3},{7,2},{8,13},{9,12},{10,... | collective-permute-start | bytes 98312 | tf_op jit(solution)/shard_map/ppermute | solution.py:27
  94.4 4.9 %collective-permute-start.37 = (bf16[128,128]{1,0:T(8,128)(2,1)S(1)}, bf16[128,128]{1,0:T(8,128)(2,1)S(1)}, u32[]{:S(2)}, u32[]{:S(2)}) collective-permute-start(bf16[128,128]{1,0:T(8,128)(2,1)S(1)} %get-tuple-element.75), channel_id=1, source_target_pairs={{0,6},{1,7},{2,4},{3,5},{4,2},{5,3},{6,0},{7,1},{8,14},{9,15},{10,... | collective-permute-start | bytes 98312 | tf_op jit(solution)/shard_map/ppermute | solution.py:27
  96.1 4.6 %collective-permute-start.38 = (bf16[128,128]{1,0:T(8,128)(2,1)S(1)}, bf16[128,128]{1,0:T(8,128)(2,1)S(1)}, u32[]{:S(2)}, u32[]{:S(2)}) collective-permute-start(bf16[128,128]{1,0:T(8,128)(2,1)S(1)} %get-tuple-element.76), channel_id=1, source_target_pairs={{0,7},{1,6},{2,5},{3,4},{4,3},{5,2},{6,1},{7,0},{8,15},{9,14},{10,... | collective-permute-start | bytes 98312 | tf_op jit(solution)/shard_map/ppermute | solution.py:27
